TPU v7x, 32 devices: a whole 2x2x4 slice. The times are simulated.
32 devices in a mesh: gx: 4 (over y, core), gy: 8 (over z, x).
Axes of the slice: x: 2, y: 2, z: 4, core: 2. Of those that a mesh axis runs over, the one named last changes fastest.
Arguments:
- displacement: float32 [3, 32, 64, 128], P(None, 'gx', 'gy'), may hold values from -0.12 to 0.12
- velocity: float32 [3, 32, 64, 128], P(None, 'gx', 'gy'), may hold values from -4 to 4
- intact: int32 [61, 32, 64, 128], P(None, 'gx', 'gy'), may hold values 0 or 1
- material: int32 [32, 64, 128], P('gx', 'gy'), may hold values from 0 to 7
- bulk_modulus: float32 [8], replicated, may hold values from 80 to 800
- shear_modulus: float32 [8], replicated, may hold values from 40 to 400
- density: float32 [8], replicated, may hold values from 1 to 4
Outputs:
- new_displacement: float32 [3, 32, 64, 128], P(None, 'gx', 'gy')
- new_velocity: float32 [3, 32, 64, 128], P(None, 'gx', 'gy')
- last_force: float32 [3, 32, 64, 128], P(None, 'gx', 'gy')
Inputs may be any that keep to these rules, and one draw needn't show every extreme that they name: intact[k, i] refers to the bond from node i to node i + e_k.
All inputs are finite; a program needn't handle non-finite values. No bound on the sum of `intact` on one device may be relied on, other than what follows from the above.
Results may differ from a plain program's by a relative error of at most 0.00002.
Values sent between devices are 32-bit elements; how exact they have to be, the bound alone decides.
A program may use at most 64 MiB of HBM per device.

v0:
```python
import math

import jax
import jax.numpy as jnp
from jax import lax
from jax.sharding import PartitionSpec as P

STEPS = 2


time_step = 0.02


def extended_2(shard, sides, width):
    for axis, dim in sides:
        size, length = (lax.axis_size(axis), shard.shape[dim])
        up = [(i, (i + 1) % size) for i in range(size - 1)]
        down = [(j, i) for i, j in up]
        last = lax.slice_in_dim(shard, length - width, length, axis=dim)
        first = lax.slice_in_dim(shard, 0, width, axis=dim)
        before = lax.ppermute(last, axis, up)
        after = lax.ppermute(first, axis, down)
        shard = jnp.concatenate([before, shard, after], axis=dim)
    return shard


def passed_along(block, axis, distance):
    devices = range(lax.axis_size(axis))
    route = [(i - distance, i) for i in devices if i - distance in devices]
    return lax.ppermute(block, axis, route)


def half_offsets():
    result = []
    for along_x in range(-3, 4):
        for along_y in range(-3, 4):
            for along_z in range(-3, 4):
                if along_x * along_x + along_y * along_y + along_z * along_z <= 9 and (
                    along_x,
                    along_y,
                    along_z,
                ) > (0, 0, 0):
                    result.append((along_x, along_y, along_z))
    return result


def weighted_volume(offsets):
    return 2.0 * sum(
        (
            math.sqrt(float(offset[0] * offset[0] + offset[1] * offset[1] + offset[2] * offset[2]))
            for offset in offsets
        )
    )


def shift_depth(values, offset):
    if offset == 0:
        return values
    tile_depth = values.shape[-1]
    zeros_block = jnp.zeros(values.shape[:-1] + (abs(offset),), values.dtype)
    if offset > 0:
        return jnp.concatenate([values[..., offset:], zeros_block], -1)
    return jnp.concatenate([zeros_block, values[..., : tile_depth + offset]], -1)


def depth_inside(tile_depth, offset):
    positions = jnp.arange(tile_depth, dtype=jnp.int32) + offset
    return ((positions >= 0) & (positions < tile_depth)).astype(jnp.float32)


def extend_upper(side_extended, upper_rows, dimension):
    return jnp.concatenate([jnp.zeros_like(upper_rows), side_extended, upper_rows], dimension)


def fold_axis(halved, dimension, margin, interior):
    region = interior + 2 * margin - 6
    middle = lax.slice_in_dim(halved, 6, 6 + region, axis=dimension)
    low_part = lax.slice_in_dim(halved, 0, margin, axis=dimension)
    high_part = lax.slice_in_dim(
        halved, halved.shape[dimension] - margin, halved.shape[dimension], axis=dimension
    )
    low_padding = [(0, 0)] * halved.ndim
    low_padding[dimension] = (0, region - margin)
    high_padding = [(0, 0)] * halved.ndim
    high_padding[dimension] = (region - margin, 0)
    return middle + jnp.pad(low_part, low_padding) + jnp.pad(high_part, high_padding)


def fold_plane(halved, dimension, margin, tile_rows, tile_columns):
    return fold_axis(
        fold_axis(halved, dimension, margin, tile_rows), dimension + 1, margin, tile_columns
    )


def class_lookup(lookup_table, classes):
    class_numbers = jnp.arange(lookup_table.shape[0], dtype=jnp.int32)[:, None, None, None]
    return jnp.sum(
        jnp.where(classes[None] == class_numbers, lookup_table[:, None, None, None], 0.0), 0
    )


def plane_inside(tile_rows, tile_columns):
    row_position = lax.axis_index("gx") * tile_rows + jnp.arange(-3, tile_rows + 3, dtype=jnp.int32)
    column_position = lax.axis_index("gy") * tile_columns + jnp.arange(
        -3, tile_columns + 3, dtype=jnp.int32
    )
    row_inside = (row_position >= 0) & (row_position < tile_rows * lax.axis_size("gx"))
    column_inside = (column_position >= 0) & (column_position < tile_columns * lax.axis_size("gy"))
    return (row_inside[:, None] & column_inside[None, :]).astype(jnp.float32)


def tile_view(extended, offset, tile_rows, tile_columns):
    window = extended[
        ...,
        3 + offset[0] : 3 + offset[0] + tile_rows,
        3 + offset[1] : 3 + offset[1] + tile_columns,
        :,
    ]
    return shift_depth(window, offset[2])


def place_back(contribution, offset):
    sliding = shift_depth(contribution, -offset[2])
    leading = [(0, 0)] * (contribution.ndim - 3)
    return jnp.pad(
        sliding, leading + [(3 + offset[0], 3 - offset[0]), (3 + offset[1], 3 - offset[1]), (0, 0)]
    )


def bond_weight(flags, inside_plane, offset, tile_rows, tile_columns, tile_depth):
    plane = inside_plane[
        3 + offset[0] : 3 + offset[0] + tile_rows, 3 + offset[1] : 3 + offset[1] + tile_columns
    ]
    return (
        flags.astype(jnp.float32)
        * plane[:, :, None]
        * depth_inside(tile_depth, offset[2])[None, None, :]
    )


def bond_state(displacement_wide, own_motion, offset, tile_rows, tile_columns):
    partner = tile_view(displacement_wide, offset, tile_rows, tile_columns)
    radius = math.sqrt(float(offset[0] * offset[0] + offset[1] * offset[1] + offset[2] * offset[2]))
    components = [offset[number] + partner[number] - own_motion[number] for number in range(3)]
    length = jnp.sqrt(
        components[0] * components[0]
        + components[1] * components[1]
        + components[2] * components[2]
    )
    return (components, length, length - radius, radius)


def strain_partial(displacement_wide, intact, inside_plane, tile_rows, tile_columns, tile_depth):
    own_motion = displacement_wide[:, 3 : 3 + tile_rows, 3 : 3 + tile_columns, :]
    own_sum = jnp.zeros((tile_rows, tile_columns, tile_depth), jnp.float32)
    spread = jnp.zeros((tile_rows + 6, tile_columns + 6, tile_depth), jnp.float32)
    for bond_index, offset in enumerate(half_offsets()):
        components, length, stretch, radius = bond_state(
            displacement_wide, own_motion, offset, tile_rows, tile_columns
        )
        contribution = (
            bond_weight(
                intact[bond_index], inside_plane, offset, tile_rows, tile_columns, tile_depth
            )
            * stretch
        )
        own_sum = own_sum + contribution
        spread = spread + place_back(contribution, offset)
    return spread + jnp.pad(own_sum, ((3, 3), (3, 3), (0, 0)))


def force_partial(
    displacement_wide,
    dilatation_wide,
    bulk_wide,
    shear_wide,
    intact,
    inside_plane,
    volume,
    tile_rows,
    tile_columns,
    tile_depth,
):
    own_motion = displacement_wide[:, 3 : 3 + tile_rows, 3 : 3 + tile_columns, :]
    pressure_wide = bulk_wide * dilatation_wide
    twisting_wide = shear_wide * dilatation_wide
    own_pressure = pressure_wide[3 : 3 + tile_rows, 3 : 3 + tile_columns, :]
    own_twisting = twisting_wide[3 : 3 + tile_rows, 3 : 3 + tile_columns, :]
    own_shear = shear_wide[3 : 3 + tile_rows, 3 : 3 + tile_columns, :]
    own_force = jnp.zeros((3, tile_rows, tile_columns, tile_depth), jnp.float32)
    spread = jnp.zeros((3, tile_rows + 6, tile_columns + 6, tile_depth), jnp.float32)
    for bond_index, offset in enumerate(half_offsets()):
        components, length, stretch, radius = bond_state(
            displacement_wide, own_motion, offset, tile_rows, tile_columns
        )
        weight = bond_weight(
            intact[bond_index], inside_plane, offset, tile_rows, tile_columns, tile_depth
        )
        tension = (
            weight
            / radius
            * (
                3.0
                * radius
                / volume
                * (own_pressure + tile_view(pressure_wide, offset, tile_rows, tile_columns))
                + 15.0
                / volume
                * (
                    (own_shear + tile_view(shear_wide, offset, tile_rows, tile_columns)) * stretch
                    - radius
                    / 3.0
                    * (own_twisting + tile_view(twisting_wide, offset, tile_rows, tile_columns))
                )
            )
        )
        vector = jnp.stack([tension * component / length for component in components])
        own_force = own_force + vector
        spread = spread - place_back(vector, offset)
    return spread + jnp.pad(own_force, ((0, 0), (3, 3), (3, 3), (0, 0)))


def return_force(pushed, tile_rows, tile_columns):
    halved = extended_2(pushed, (("gx", 1), ("gy", 2)), 3)
    return fold_plane(halved, 1, 3, tile_rows, tile_columns)


def on_device(displacement, velocity, intact, material, bulk_modulus, shear_modulus, density):
    tile_rows, tile_columns, tile_depth = material.shape
    volume = weighted_volume(half_offsets())
    classes_side = extended_2(material, (("gy", 1),), 3)
    classes_next = passed_along(classes_side[:3], "gx", -1)
    classes_wide = extend_upper(classes_side, classes_next, 0)
    bulk_wide = class_lookup(bulk_modulus, classes_wide)
    shear_wide = class_lookup(shear_modulus, classes_wide)
    inertia_wide = class_lookup(density, classes_wide)
    inertia_tile = inertia_wide[3 : 3 + tile_rows, 3 : 3 + tile_columns, :]
    inside_plane = plane_inside(tile_rows, tile_columns)
    forces = jnp.zeros(displacement.shape, jnp.float32)
    state_side = extended_2(jnp.concatenate([displacement, velocity], 0), (("gy", 2),), 3)
    state_next = passed_along(state_side[:, :3], "gx", -1)
    state_wide = extend_upper(state_side, state_next, 1)
    displacement_wide = state_wide[:3]
    velocity_wide = state_wide[3:]
    for counter in range(STEPS):
        partial_value = strain_partial(
            displacement_wide, intact, inside_plane, tile_rows, tile_columns, tile_depth
        )
        returned = extended_2(partial_value, (("gx", 0), ("gy", 1)), 6)
        dilatation_wide = 3.0 / volume * fold_plane(returned, 0, 6, tile_rows, tile_columns)
        pushed = force_partial(
            displacement_wide,
            dilatation_wide,
            bulk_wide,
            shear_wide,
            intact,
            inside_plane,
            volume,
            tile_rows,
            tile_columns,
            tile_depth,
        )
        if counter + 1 < STEPS:
            spread_back = extended_2(pushed, (("gx", 1), ("gy", 2)), 6)
            forces_wide = fold_plane(spread_back, 1, 6, tile_rows, tile_columns)
            velocity_wide = velocity_wide + time_step * forces_wide / inertia_wide
            displacement_wide = displacement_wide + time_step * velocity_wide
        else:
            forces = return_force(pushed, tile_rows, tile_columns)
            velocity = (
                velocity_wide[:, 3 : 3 + tile_rows, 3 : 3 + tile_columns, :]
                + time_step * forces / inertia_tile
            )
            displacement = (
                displacement_wide[:, 3 : 3 + tile_rows, 3 : 3 + tile_columns, :]
                + time_step * velocity
            )
    return (displacement, velocity, forces)


def solution(mesh):
    return jax.shard_map(
        on_device,
        mesh=mesh,
        in_specs=(
            P(None, "gx", "gy", None),
            P(None, "gx", "gy", None),
            P(None, "gx", "gy", None),
            P("gx", "gy", None),
            P(),
            P(),
            P(),
        ),
        out_specs=(P(None, "gx", "gy", None), P(None, "gx", "gy", None), P(None, "gx", "gy", None)),
        check_vma=False,
    )
```

profile of v0, /device:TPU:9, one launch (start us, length us, event | category | flops | bytes accessed | tf_op | source)
XLA Modules:
  0.0 154.8 jit_solution(2076999402524175350)
XLA Ops:
  0.6 0.9 constant_dynamic-update-slice_fusion.1
  1.5 0.9 constant_dynamic-update-slice_fusion
  2.5 3.0 %collective-permute-start.1 = (f32[6,8,3,128]{3,2,1,0:T(4,128)S(1)}, f32[6,8,3,128]{3,2,1,0:T(4,128)S(1)}, u32[]{:S(2)}, u32[]{:S(2)}) collective-permute-start(f32[6,8,3,128]{3,2,1,0:T(4,128)S(1)} %get-tuple-element.968), channel_id=1, source_target_pairs={{1,0},{2,1},{3,2},{4,3},{5,4},{6,5},{7,6},{9,8},{10,9},{11,10},{12... | collective-permute-start | bytes 221192 | tf_op jit(solution)/shard_map/ppermute | solution.py:22
  5.5 2.3 %collective-permute-start = (f32[6,8,3,128]{3,2,1,0:T(4,128)S(1)}, f32[6,8,3,128]{3,2,1,0:T(4,128)S(1)}, u32[]{:S(2)}, u32[]{:S(2)}) collective-permute-start(f32[6,8,3,128]{3,2,1,0:T(4,128)S(1)} %get-tuple-element.967), channel_id=1, source_target_pairs={{0,1},{1,2},{2,3},{3,4},{4,5},{5,6},{6,7},{8,9},{9,10},{10,11},{11... | collective-permute-start | bytes 221192 | tf_op jit(solution)/shard_map/ppermute | solution.py:21
  7.8 0.8 fusion.1345
  8.6 4.0 %collective-permute-start.3 = (s32[8,3,128]{2,1,0:T(4,128)S(1)}, s32[8,3,128]{2,1,0:T(4,128)S(1)}, u32[]{:S(2)}, u32[]{:S(2)}) collective-permute-start(s32[8,3,128]{2,1,0:T(4,128)S(1)} %get-tuple-element.1298), channel_id=1, source_target_pairs={{0,1},{1,2},{2,3},{3,4},{4,5},{5,6},{6,7},{8,9},{9,10},{10,11},{11... | collective-permute-start | bytes 36872 | tf_op jit(solution)/shard_map/ppermute | solution.py:21
  12.6 2.2 %collective-permute-start.4 = (s32[8,3,128]{2,1,0:T(4,128)S(1)}, s32[8,3,128]{2,1,0:T(4,128)S(1)}, u32[]{:S(2)}, u32[]{:S(2)}) collective-permute-start(s32[8,3,128]{2,1,0:T(4,128)S(1)} %get-tuple-element.1299), channel_id=1, source_target_pairs={{1,0},{2,1},{3,2},{4,3},{5,4},{6,5},{7,6},{9,8},{10,9},{11,10},{12... | collective-permute-start | bytes 36872 | tf_op jit(solution)/shard_map/ppermute | solution.py:22
  15.0 2.1 %collective-permute-done.4 = s32[8,3,128]{2,1,0:T(4,128)S(1)} collective-permute-done((s32[8,3,128]{2,1,0:T(4,128)S(1)}, s32[8,3,128]{2,1,0:T(4,128)S(1)}, u32[]{:S(2)}, u32[]{:S(2)}) %collective-permute-start.4) | collective-permute-done | bytes 12320 | tf_op jit(solution)/shard_map/ppermute | solution.py:22
  17.1 0.7 pad_add_fusion.140
  17.8 4.6 %collective-permute-start.5 = (s32[3,14,128]{2,1,0:T(8,128)S(1)}, s32[3,14,128]{2,1,0:T(8,128)S(1)}, u32[]{:S(2)}, u32[]{:S(2)}) collective-permute-start(s32[3,14,128]{2,1,0:T(8,128)S(1)} %pad_add_fusion.140), channel_id=1, source_target_pairs={{8,0},{16,8},{24,16},{9,1},{17,9},{25,17},{10,2},{18,10},{26,18},{... | collective-permute-start | bytes 64520 | tf_op jit(solution)/shard_map/ppermute | solution.py:30
  22.4 1.0 slice.2676
  23.4 1.0 slice.2685
  24.4 1.0 slice.2691
  25.4 0.8 pad_add_fusion.92
  26.2 1.5 select_reduce_fusion
  28.1 1.9 %collective-permute-start.2 = (f32[6,3,14,128]{3,2,1,0:T(8,128)S(1)}, f32[6,3,14,128]{3,2,1,0:T(8,128)S(1)}, u32[]{:S(2)}, u32[]{:S(2)}) collective-permute-start(f32[6,3,14,128]{3,2,1,0:T(8,128)S(1)} %pad_maximum_fusion.9), channel_id=1, source_target_pairs={{8,0},{16,8},{24,16},{9,1},{17,9},{25,17},{10,2},{18,10},{26,18},{... | collective-permute-start | bytes 387080 | tf_op jit(solution)/shard_map/ppermute | solution.py:30
  30.0 0.2 fusion.101
  30.2 0.2 fusion.100
  30.4 4.2 %collective-permute-done.2 = f32[6,3,14,128]{3,2,1,0:T(8,128)S(1)} collective-permute-done((f32[6,3,14,128]{3,2,1,0:T(8,128)S(1)}, f32[6,3,14,128]{3,2,1,0:T(8,128)S(1)}, u32[]{:S(2)}, u32[]{:S(2)}) %collective-permute-start.2) | collective-permute-done | bytes 129056 | tf_op jit(solution)/shard_map/ppermute | solution.py:30
  34.7 0.4 fusion.1312
  35.1 0.3 fusion.1313
  35.4 0.6 copy-done
  35.9 0.7 copy-done.1
  36.6 2.2 %add_add_fusion.3 = (f32[8,8,128]{2,1,0:T(8,128)S(1)}, f32[8,8,128]{2,1,0:T(8,128)S(1)}, f32[8,8,128]{2,1,0:T(8,128)S(1)}, f32[8,8,128]{2,1,0:T(8,128)S(1)}, f32...) fusion(f32[128]{0:T(128)S(1)} %get-tuple-element.1318, ...), kind=kLoop, calls=%fused_computation.2719 | loop fusion | flops 8216576 | bytes 12085504 | tf_op jit(solution)/shard_map/add | solution.py:167
  40.6 0.6 fusion.80
  41.2 1.9 %collective-permute-start.6 = (f32[6,14,128]{2,1,0:T(8,128)S(1)}, f32[6,14,128]{2,1,0:T(8,128)S(1)}, u32[]{:S(2)}, u32[]{:S(2)}) collective-permute-start(f32[6,14,128]{2,1,0:T(8,128)S(1)} %get-tuple-element.1201), channel_id=1, source_target_pairs={{0,8},{8,16},{16,24},{1,9},{9,17},{17,25},{2,10},{10,18},{18,26},{... | collective-permute-start | bytes 129032 | tf_op jit(solution)/shard_map/ppermute | solution.py:21
  43.2 2.4 %collective-permute-start.7 = (f32[6,14,128]{2,1,0:T(8,128)S(1)}, f32[6,14,128]{2,1,0:T(8,128)S(1)}, u32[]{:S(2)}, u32[]{:S(2)}) collective-permute-start(f32[6,14,128]{2,1,0:T(8,128)S(1)} %get-tuple-element.1202), channel_id=1, source_target_pairs={{8,0},{16,8},{24,16},{9,1},{17,9},{25,17},{10,2},{18,10},{26,18},{... | collective-permute-start | bytes 129032 | tf_op jit(solution)/shard_map/ppermute | solution.py:22
  45.7 2.9 %collective-permute-done.7 = f32[6,14,128]{2,1,0:T(8,128)S(1)} collective-permute-done((f32[6,14,128]{2,1,0:T(8,128)S(1)}, f32[6,14,128]{2,1,0:T(8,128)S(1)}, u32[]{:S(2)}, u32[]{:S(2)}) %collective-permute-start.7) | collective-permute-done | bytes 43040 | tf_op jit(solution)/shard_map/ppermute | solution.py:22
  48.6 3.2 %collective-permute-start.8 = (f32[26,6,128]{2,1,0:T(8,128)S(1)}, f32[26,6,128]{2,1,0:T(8,128)S(1)}, u32[]{:S(2)}, u32[]{:S(2)}) collective-permute-start(f32[26,6,128]{2,1,0:T(8,128)S(1)} %get-tuple-element.965), channel_id=1, source_target_pairs={{0,1},{1,2},{2,3},{3,4},{4,5},{5,6},{6,7},{8,9},{9,10},{10,11},{11... | collective-permute-start | bytes 239624 | tf_op jit(solution)/shard_map/ppermute | solution.py:21
  51.8 3.2 %collective-permute-start.9 = (f32[26,6,128]{2,1,0:T(8,128)S(1)}, f32[26,6,128]{2,1,0:T(8,128)S(1)}, u32[]{:S(2)}, u32[]{:S(2)}) collective-permute-start(f32[26,6,128]{2,1,0:T(8,128)S(1)} %get-tuple-element.966), channel_id=1, source_target_pairs={{1,0},{2,1},{3,2},{4,3},{5,4},{6,5},{7,6},{9,8},{10,9},{11,10},{12... | collective-permute-start | bytes 239624 | tf_op jit(solution)/shard_map/ppermute | solution.py:22
  55.2 2.2 %collective-permute-done.9 = f32[26,6,128]{2,1,0:T(8,128)S(1)} collective-permute-done((f32[26,6,128]{2,1,0:T(8,128)S(1)}, f32[26,6,128]{2,1,0:T(8,128)S(1)}, u32[]{:S(2)}, u32[]{:S(2)}) %collective-permute-start.9) | collective-permute-done | bytes 79904 | tf_op jit(solution)/shard_map/ppermute | solution.py:22
  66.6 0.6 add_add_fusion.1
  69.3 1.7 %fusion.28 = f32[3,14,14,128]{3,2,1,0:T(8,128)S(1)} fusion(f32[3,8,8,127]{3,2,1,0:T(8,128)S(1)} %bitcast.4315, f32[3,8,8,127]{3,2,1,0:T(8,128)S(1)} %slice.7436, f32[3,8,8,126]{3,2,1,0:T(8,128)S(1)} %bitcast.4313, f32[3,8,8,127]{3,2,1,0:T(8,128)S(1)} %bitcast.4311, f32[3,8,8,127]{3,2,1,0:T(8,128)S(1)} %slice.7421, f32[3,8,8,126]{3,2,1,0:T(8,128)S(1)} %slice.7417, ...), kind=kLoop, calls=%fused_computation.124 | loop fusion | flops 4666368 | bytes 6342144 | tf_op jit(solution)/shard_map/add | solution.py:220
  71.1 3.2 %collective-permute-start.10 = (f32[3,6,14,128]{3,2,1,0:T(8,128)S(1)}, f32[3,6,14,128]{3,2,1,0:T(8,128)S(1)}, u32[]{:S(2)}, u32[]{:S(2)}) collective-permute-start(f32[3,6,14,128]{3,2,1,0:T(8,128)S(1)} %get-tuple-element.855), channel_id=1, source_target_pairs={{0,8},{8,16},{16,24},{1,9},{9,17},{17,25},{2,10},{10,18},{18,26},{... | collective-permute-start | bytes 387080 | tf_op jit(solution)/shard_map/ppermute | solution.py:21
  74.3 1.9 %collective-permute-start.11 = (f32[3,6,14,128]{3,2,1,0:T(8,128)S(1)}, f32[3,6,14,128]{3,2,1,0:T(8,128)S(1)}, u32[]{:S(2)}, u32[]{:S(2)}) collective-permute-start(f32[3,6,14,128]{3,2,1,0:T(8,128)S(1)} %get-tuple-element.856), channel_id=1, source_target_pairs={{8,0},{16,8},{24,16},{9,1},{17,9},{25,17},{10,2},{18,10},{26,18},{... | collective-permute-start | bytes 387080 | tf_op jit(solution)/shard_map/ppermute | solution.py:22
  76.4 4.4 %collective-permute-done.11 = f32[3,6,14,128]{3,2,1,0:T(8,128)S(1)} collective-permute-done((f32[3,6,14,128]{3,2,1,0:T(8,128)S(1)}, f32[3,6,14,128]{3,2,1,0:T(8,128)S(1)}, u32[]{:S(2)}, u32[]{:S(2)}) %collective-permute-start.11) | collective-permute-done | bytes 129056 | tf_op jit(solution)/shard_map/ppermute | solution.py:22
  80.9 4.0 %collective-permute-start.12 = (f32[3,26,6,128]{3,2,1,0:T(8,128)S(1)}, f32[3,26,6,128]{3,2,1,0:T(8,128)S(1)}, u32[]{:S(2)}, u32[]{:S(2)}) collective-permute-start(f32[3,26,6,128]{3,2,1,0:T(8,128)S(1)} %get-tuple-element.491), channel_id=1, source_target_pairs={{0,1},{1,2},{2,3},{3,4},{4,5},{5,6},{6,7},{8,9},{9,10},{10,11},{11... | collective-permute-start | bytes 718856 | tf_op jit(solution)/shard_map/ppermute | solution.py:21
  84.9 2.4 %collective-permute-start.13 = (f32[3,26,6,128]{3,2,1,0:T(8,128)S(1)}, f32[3,26,6,128]{3,2,1,0:T(8,128)S(1)}, u32[]{:S(2)}, u32[]{:S(2)}) collective-permute-start(f32[3,26,6,128]{3,2,1,0:T(8,128)S(1)} %get-tuple-element.492), channel_id=1, source_target_pairs={{1,0},{2,1},{3,2},{4,3},{5,4},{6,5},{7,6},{9,8},{10,9},{11,10},{12... | collective-permute-start | bytes 718856 | tf_op jit(solution)/shard_map/ppermute | solution.py:22
  87.4 8.9 %collective-permute-done.12 = f32[3,26,6,128]{3,2,1,0:T(8,128)S(1)} collective-permute-done((f32[3,26,6,128]{3,2,1,0:T(8,128)S(1)}, f32[3,26,6,128]{3,2,1,0:T(8,128)S(1)}, u32[]{:S(2)}, u32[]{:S(2)}) %collective-permute-start.12) | collective-permute-done | bytes 239648 | tf_op jit(solution)/shard_map/ppermute | solution.py:21
  96.3 0.9 collective-permute-done.13
  97.2 0.2 pad_maximum_fusion
  97.6 0.2 slice_add_fusion
  97.8 0.4 fusion.1315
  98.2 0.4 fusion.1316
  99.3 0.2 add_sqrt_fusion.8
  100.1 2.0 %add_add_fusion.2 = (f32[8,8,128]{2,1,0:T(8,128)S(1)}, f32[8,8,128]{2,1,0:T(8,128)S(1)}, f32[8,8,128]{2,1,0:T(8,128)S(1)}, f32[8,8,128]{2,1,0:T(8,128)S(1)}, f32...) fusion(f32[128]{0:T(128)S(1)} %get-tuple-element.1318, ...), kind=kLoop, calls=%fused_computation.2380 | loop fusion | flops 5324800 | bytes 8967680 | tf_op jit(solution)/shard_map/add | solution.py:167
  103.8 0.6 fusion.62
  104.4 1.9 %collective-permute-start.14 = (f32[6,14,128]{2,1,0:T(8,128)S(1)}, f32[6,14,128]{2,1,0:T(8,128)S(1)}, u32[]{:S(2)}, u32[]{:S(2)}) collective-permute-start(f32[6,14,128]{2,1,0:T(8,128)S(1)} %get-tuple-element.1061), channel_id=1, source_target_pairs={{0,8},{8,16},{16,24},{1,9},{9,17},{17,25},{2,10},{10,18},{18,26},{... | collective-permute-start | bytes 129032 | tf_op jit(solution)/shard_map/ppermute | solution.py:21
  106.3 2.4 %collective-permute-start.15 = (f32[6,14,128]{2,1,0:T(8,128)S(1)}, f32[6,14,128]{2,1,0:T(8,128)S(1)}, u32[]{:S(2)}, u32[]{:S(2)}) collective-permute-start(f32[6,14,128]{2,1,0:T(8,128)S(1)} %get-tuple-element.1062), channel_id=1, source_target_pairs={{8,0},{16,8},{24,16},{9,1},{17,9},{25,17},{10,2},{18,10},{26,18},{... | collective-permute-start | bytes 129032 | tf_op jit(solution)/shard_map/ppermute | solution.py:22
  108.7 3.0 %collective-permute-done.15 = f32[6,14,128]{2,1,0:T(8,128)S(1)} collective-permute-done((f32[6,14,128]{2,1,0:T(8,128)S(1)}, f32[6,14,128]{2,1,0:T(8,128)S(1)}, u32[]{:S(2)}, u32[]{:S(2)}) %collective-permute-start.15) | collective-permute-done | bytes 43040 | tf_op jit(solution)/shard_map/ppermute | solution.py:22
  111.8 2.9 %collective-permute-start.16 = (f32[26,6,128]{2,1,0:T(8,128)S(1)}, f32[26,6,128]{2,1,0:T(8,128)S(1)}, u32[]{:S(2)}, u32[]{:S(2)}) collective-permute-start(f32[26,6,128]{2,1,0:T(8,128)S(1)} %get-tuple-element.963), channel_id=1, source_target_pairs={{0,1},{1,2},{2,3},{3,4},{4,5},{5,6},{6,7},{8,9},{9,10},{10,11},{11... | collective-permute-start | bytes 239624 | tf_op jit(solution)/shard_map/ppermute | solution.py:21
  114.7 3.3 %collective-permute-start.17 = (f32[26,6,128]{2,1,0:T(8,128)S(1)}, f32[26,6,128]{2,1,0:T(8,128)S(1)}, u32[]{:S(2)}, u32[]{:S(2)}) collective-permute-start(f32[26,6,128]{2,1,0:T(8,128)S(1)} %get-tuple-element.964), channel_id=1, source_target_pairs={{1,0},{2,1},{3,2},{4,3},{5,4},{6,5},{7,6},{9,8},{10,9},{11,10},{12... | collective-permute-start | bytes 239624 | tf_op jit(solution)/shard_map/ppermute | solution.py:22
  118.0 0.2 collective-permute-done.16
  118.1 2.3 %collective-permute-done.17 = f32[26,6,128]{2,1,0:T(8,128)S(1)} collective-permute-done((f32[26,6,128]{2,1,0:T(8,128)S(1)}, f32[26,6,128]{2,1,0:T(8,128)S(1)}, u32[]{:S(2)}, u32[]{:S(2)}) %collective-permute-start.17) | collective-permute-done | bytes 79904 | tf_op jit(solution)/shard_map/ppermute | solution.py:22
  130.5 0.6 add_add_fusion
  133.2 1.7 %fusion.8 = f32[3,14,14,128]{3,2,1,0:T(8,128)S(1)} fusion(f32[3,8,8,127]{3,2,1,0:T(8,128)S(1)} %bitcast.4316, f32[3,8,8,127]{3,2,1,0:T(8,128)S(1)} %slice.7769, f32[3,8,8,126]{3,2,1,0:T(8,128)S(1)} %bitcast.4314, f32[3,8,8,127]{3,2,1,0:T(8,128)S(1)} %bitcast.4312, f32[3,8,8,127]{3,2,1,0:T(8,128)S(1)} %slice.7758, f32[3,8,8,126]{3,2,1,0:T(8,128)S(1)} %slice.7755, ...), kind=kLoop, calls=%fused_computation.56 | loop fusion | flops 4666368 | bytes 6342144 | tf_op jit(solution)/shard_map/add | solution.py:220
  135.0 3.1 %collective-permute-start.18 = (f32[3,3,14,128]{3,2,1,0:T(8,128)S(1)}, f32[3,3,14,128]{3,2,1,0:T(8,128)S(1)}, u32[]{:S(2)}, u32[]{:S(2)}) collective-permute-start(f32[3,3,14,128]{3,2,1,0:T(8,128)S(1)} %get-tuple-element.735), channel_id=1, source_target_pairs={{0,8},{8,16},{16,24},{1,9},{9,17},{17,25},{2,10},{10,18},{18,26},{... | collective-permute-start | bytes 193544 | tf_op jit(solution)/shard_map/ppermute | solution.py:21
  138.1 1.9 %collective-permute-start.19 = (f32[3,3,14,128]{3,2,1,0:T(8,128)S(1)}, f32[3,3,14,128]{3,2,1,0:T(8,128)S(1)}, u32[]{:S(2)}, u32[]{:S(2)}) collective-permute-start(f32[3,3,14,128]{3,2,1,0:T(8,128)S(1)} %get-tuple-element.736), channel_id=1, source_target_pairs={{8,0},{16,8},{24,16},{9,1},{17,9},{25,17},{10,2},{18,10},{26,18},{... | collective-permute-start | bytes 193544 | tf_op jit(solution)/shard_map/ppermute | solution.py:22
  140.0 3.7 %collective-permute-done.19 = f32[3,3,14,128]{3,2,1,0:T(8,128)S(1)} collective-permute-done((f32[3,3,14,128]{3,2,1,0:T(8,128)S(1)}, f32[3,3,14,128]{3,2,1,0:T(8,128)S(1)}, u32[]{:S(2)}, u32[]{:S(2)}) %collective-permute-start.19) | collective-permute-done | bytes 64544 | tf_op jit(solution)/shard_map/ppermute | solution.py:22
  143.8 4.3 %collective-permute-start.20 = (f32[3,20,3,128]{3,2,1,0:T(4,128)S(1)}, f32[3,20,3,128]{3,2,1,0:T(4,128)S(1)}, u32[]{:S(2)}, u32[]{:S(2)}) collective-permute-start(f32[3,20,3,128]{3,2,1,0:T(4,128)S(1)} %get-tuple-element.642), channel_id=1, source_target_pairs={{0,1},{1,2},{2,3},{3,4},{4,5},{5,6},{6,7},{8,9},{9,10},{10,11},{11... | collective-permute-start | bytes 276488 | tf_op jit(solution)/shard_map/ppermute | solution.py:21
  148.1 1.9 %collective-permute-start.21 = (f32[3,20,3,128]{3,2,1,0:T(4,128)S(1)}, f32[3,20,3,128]{3,2,1,0:T(4,128)S(1)}, u32[]{:S(2)}, u32[]{:S(2)}) collective-permute-start(f32[3,20,3,128]{3,2,1,0:T(4,128)S(1)} %get-tuple-element.643), channel_id=1, source_target_pairs={{1,0},{2,1},{3,2},{4,3},{5,4},{6,5},{7,6},{9,8},{10,9},{11,10},{12... | collective-permute-start | bytes 276488 | tf_op jit(solution)/shard_map/ppermute | solution.py:22
  150.0 1.2 collective-permute-done.20
  151.2 2.5 %collective-permute-done.21 = f32[3,20,3,128]{3,2,1,0:T(4,128)S(1)} collective-permute-done((f32[3,20,3,128]{3,2,1,0:T(4,128)S(1)}, f32[3,20,3,128]{3,2,1,0:T(4,128)S(1)}, u32[]{:S(2)}, u32[]{:S(2)}) %collective-permute-start.21) | collective-permute-done | bytes 92192 | tf_op jit(solution)/shard_map/ppermute | solution.py:22
  153.9 0.8 slice_add_fusion.2
  (437 shorter events, 28.2 us)
Async XLA Ops:
  2.5 25.6 %collective-permute-start.1 = (f32[6,8,3,128]{3,2,1,0:T(4,128)S(1)}, f32[6,8,3,128]{3,2,1,0:T(4,128)S(1)}, u32[]{:S(2)}, u32[]{:S(2)}) collective-permute-start(f32[6,8,3,128]{3,2,1,0:T(4,128)S(1)} %get-tuple-element.968), channel_id=1, source_target_pairs={{1,0},{2,1},{3,2},{4,3},{5,4},{6,5},{7,6},{9,8},{10,9},{11,10},{12... | collective-permute-start | bytes 221192 | tf_op jit(solution)/shard_map/ppermute | solution.py:22
  5.5 22.6 %collective-permute-start = (f32[6,8,3,128]{3,2,1,0:T(4,128)S(1)}, f32[6,8,3,128]{3,2,1,0:T(4,128)S(1)}, u32[]{:S(2)}, u32[]{:S(2)}) collective-permute-start(f32[6,8,3,128]{3,2,1,0:T(4,128)S(1)} %get-tuple-element.967), channel_id=1, source_target_pairs={{0,1},{1,2},{2,3},{3,4},{4,5},{5,6},{6,7},{8,9},{9,10},{10,11},{11... | collective-permute-start | bytes 221192 | tf_op jit(solution)/shard_map/ppermute | solution.py:21
  8.6 6.4 %collective-permute-start.3 = (s32[8,3,128]{2,1,0:T(4,128)S(1)}, s32[8,3,128]{2,1,0:T(4,128)S(1)}, u32[]{:S(2)}, u32[]{:S(2)}) collective-permute-start(s32[8,3,128]{2,1,0:T(4,128)S(1)} %get-tuple-element.1298), channel_id=1, source_target_pairs={{0,1},{1,2},{2,3},{3,4},{4,5},{5,6},{6,7},{8,9},{9,10},{10,11},{11... | collective-permute-start | bytes 36872 | tf_op jit(solution)/shard_map/ppermute | solution.py:21
  12.6 4.5 %collective-permute-start.4 = (s32[8,3,128]{2,1,0:T(4,128)S(1)}, s32[8,3,128]{2,1,0:T(4,128)S(1)}, u32[]{:S(2)}, u32[]{:S(2)}) collective-permute-start(s32[8,3,128]{2,1,0:T(4,128)S(1)} %get-tuple-element.1299), channel_id=1, source_target_pairs={{1,0},{2,1},{3,2},{4,3},{5,4},{6,5},{7,6},{9,8},{10,9},{11,10},{12... | collective-permute-start | bytes 36872 | tf_op jit(solution)/shard_map/ppermute | solution.py:22
  17.8 7.6 %collective-permute-start.5 = (s32[3,14,128]{2,1,0:T(8,128)S(1)}, s32[3,14,128]{2,1,0:T(8,128)S(1)}, u32[]{:S(2)}, u32[]{:S(2)}) collective-permute-start(s32[3,14,128]{2,1,0:T(8,128)S(1)} %pad_add_fusion.140), channel_id=1, source_target_pairs={{8,0},{16,8},{24,16},{9,1},{17,9},{25,17},{10,2},{18,10},{26,18},{... | collective-permute-start | bytes 64520 | tf_op jit(solution)/shard_map/ppermute | solution.py:30
  28.1 6.5 %collective-permute-start.2 = (f32[6,3,14,128]{3,2,1,0:T(8,128)S(1)}, f32[6,3,14,128]{3,2,1,0:T(8,128)S(1)}, u32[]{:S(2)}, u32[]{:S(2)}) collective-permute-start(f32[6,3,14,128]{3,2,1,0:T(8,128)S(1)} %pad_maximum_fusion.9), channel_id=1, source_target_pairs={{8,0},{16,8},{24,16},{9,1},{17,9},{25,17},{10,2},{18,10},{26,18},{... | collective-permute-start | bytes 387080 | tf_op jit(solution)/shard_map/ppermute | solution.py:30
  35.0 0.9 copy-start
  35.0 1.6 %copy-start.1 = (s32[61,8,8,128]{3,2,1,0:T(8,128)S(1)}, s32[61,8,8,128]{3,2,1,0:T(8,128)}, u32[]{:S(2)}) copy-start(s32[61,8,8,128]{3,2,1,0:T(8,128)} %param.9) | copy-start | bytes 5996548
  40.6 16.8 %copy-start.2 = (pred[14]{0:T(512)(128)(4,1)S(1)}, pred[14]{0:T(512)(128)(4,1)}, u32[]{:S(2)}) copy-start(pred[14]{0:T(512)(128)(4,1)} %constant.273.clone.1) | copy-start | bytes 46
  41.2 4.4 %collective-permute-start.6 = (f32[6,14,128]{2,1,0:T(8,128)S(1)}, f32[6,14,128]{2,1,0:T(8,128)S(1)}, u32[]{:S(2)}, u32[]{:S(2)}) collective-permute-start(f32[6,14,128]{2,1,0:T(8,128)S(1)} %get-tuple-element.1201), channel_id=1, source_target_pairs={{0,8},{8,16},{16,24},{1,9},{9,17},{17,25},{2,10},{10,18},{18,26},{... | collective-permute-start | bytes 129032 | tf_op jit(solution)/shard_map/ppermute | solution.py:21
  43.2 5.4 %collective-permute-start.7 = (f32[6,14,128]{2,1,0:T(8,128)S(1)}, f32[6,14,128]{2,1,0:T(8,128)S(1)}, u32[]{:S(2)}, u32[]{:S(2)}) collective-permute-start(f32[6,14,128]{2,1,0:T(8,128)S(1)} %get-tuple-element.1202), channel_id=1, source_target_pairs={{8,0},{16,8},{24,16},{9,1},{17,9},{25,17},{10,2},{18,10},{26,18},{... | collective-permute-start | bytes 129032 | tf_op jit(solution)/shard_map/ppermute | solution.py:22
  48.6 6.5 %collective-permute-start.8 = (f32[26,6,128]{2,1,0:T(8,128)S(1)}, f32[26,6,128]{2,1,0:T(8,128)S(1)}, u32[]{:S(2)}, u32[]{:S(2)}) collective-permute-start(f32[26,6,128]{2,1,0:T(8,128)S(1)} %get-tuple-element.965), channel_id=1, source_target_pairs={{0,1},{1,2},{2,3},{3,4},{4,5},{5,6},{6,7},{8,9},{9,10},{10,11},{11... | collective-permute-start | bytes 239624 | tf_op jit(solution)/shard_map/ppermute | solution.py:21
  51.8 5.5 %collective-permute-start.9 = (f32[26,6,128]{2,1,0:T(8,128)S(1)}, f32[26,6,128]{2,1,0:T(8,128)S(1)}, u32[]{:S(2)}, u32[]{:S(2)}) collective-permute-start(f32[26,6,128]{2,1,0:T(8,128)S(1)} %get-tuple-element.966), channel_id=1, source_target_pairs={{1,0},{2,1},{3,2},{4,3},{5,4},{6,5},{7,6},{9,8},{10,9},{11,10},{12... | collective-permute-start | bytes 239624 | tf_op jit(solution)/shard_map/ppermute | solution.py:22
  71.1 5.3 %collective-permute-start.10 = (f32[3,6,14,128]{3,2,1,0:T(8,128)S(1)}, f32[3,6,14,128]{3,2,1,0:T(8,128)S(1)}, u32[]{:S(2)}, u32[]{:S(2)}) collective-permute-start(f32[3,6,14,128]{3,2,1,0:T(8,128)S(1)} %get-tuple-element.855), channel_id=1, source_target_pairs={{0,8},{8,16},{16,24},{1,9},{9,17},{17,25},{2,10},{10,18},{18,26},{... | collective-permute-start | bytes 387080 | tf_op jit(solution)/shard_map/ppermute | solution.py:21
  74.3 6.5 %collective-permute-start.11 = (f32[3,6,14,128]{3,2,1,0:T(8,128)S(1)}, f32[3,6,14,128]{3,2,1,0:T(8,128)S(1)}, u32[]{:S(2)}, u32[]{:S(2)}) collective-permute-start(f32[3,6,14,128]{3,2,1,0:T(8,128)S(1)} %get-tuple-element.856), channel_id=1, source_target_pairs={{8,0},{16,8},{24,16},{9,1},{17,9},{25,17},{10,2},{18,10},{26,18},{... | collective-permute-start | bytes 387080 | tf_op jit(solution)/shard_map/ppermute | solution.py:22
  80.9 15.5 %collective-permute-start.12 = (f32[3,26,6,128]{3,2,1,0:T(8,128)S(1)}, f32[3,26,6,128]{3,2,1,0:T(8,128)S(1)}, u32[]{:S(2)}, u32[]{:S(2)}) collective-permute-start(f32[3,26,6,128]{3,2,1,0:T(8,128)S(1)} %get-tuple-element.491), channel_id=1, source_target_pairs={{0,1},{1,2},{2,3},{3,4},{4,5},{5,6},{6,7},{8,9},{9,10},{10,11},{11... | collective-permute-start | bytes 718856 | tf_op jit(solution)/shard_map/ppermute | solution.py:21
  84.9 12.3 %collective-permute-start.13 = (f32[3,26,6,128]{3,2,1,0:T(8,128)S(1)}, f32[3,26,6,128]{3,2,1,0:T(8,128)S(1)}, u32[]{:S(2)}, u32[]{:S(2)}) collective-permute-start(f32[3,26,6,128]{3,2,1,0:T(8,128)S(1)} %get-tuple-element.492), channel_id=1, source_target_pairs={{1,0},{2,1},{3,2},{4,3},{5,4},{6,5},{7,6},{9,8},{10,9},{11,10},{12... | collective-permute-start | bytes 718856 | tf_op jit(solution)/shard_map/ppermute | solution.py:22
  104.4 4.3 %collective-permute-start.14 = (f32[6,14,128]{2,1,0:T(8,128)S(1)}, f32[6,14,128]{2,1,0:T(8,128)S(1)}, u32[]{:S(2)}, u32[]{:S(2)}) collective-permute-start(f32[6,14,128]{2,1,0:T(8,128)S(1)} %get-tuple-element.1061), channel_id=1, source_target_pairs={{0,8},{8,16},{16,24},{1,9},{9,17},{17,25},{2,10},{10,18},{18,26},{... | collective-permute-start | bytes 129032 | tf_op jit(solution)/shard_map/ppermute | solution.py:21
  106.3 5.4 %collective-permute-start.15 = (f32[6,14,128]{2,1,0:T(8,128)S(1)}, f32[6,14,128]{2,1,0:T(8,128)S(1)}, u32[]{:S(2)}, u32[]{:S(2)}) collective-permute-start(f32[6,14,128]{2,1,0:T(8,128)S(1)} %get-tuple-element.1062), channel_id=1, source_target_pairs={{8,0},{16,8},{24,16},{9,1},{17,9},{25,17},{10,2},{18,10},{26,18},{... | collective-permute-start | bytes 129032 | tf_op jit(solution)/shard_map/ppermute | solution.py:22
  111.8 6.4 %collective-permute-start.16 = (f32[26,6,128]{2,1,0:T(8,128)S(1)}, f32[26,6,128]{2,1,0:T(8,128)S(1)}, u32[]{:S(2)}, u32[]{:S(2)}) collective-permute-start(f32[26,6,128]{2,1,0:T(8,128)S(1)} %get-tuple-element.963), channel_id=1, source_target_pairs={{0,1},{1,2},{2,3},{3,4},{4,5},{5,6},{6,7},{8,9},{9,10},{10,11},{11... | collective-permute-start | bytes 239624 | tf_op jit(solution)/shard_map/ppermute | solution.py:21
  114.7 5.7 %collective-permute-start.17 = (f32[26,6,128]{2,1,0:T(8,128)S(1)}, f32[26,6,128]{2,1,0:T(8,128)S(1)}, u32[]{:S(2)}, u32[]{:S(2)}) collective-permute-start(f32[26,6,128]{2,1,0:T(8,128)S(1)} %get-tuple-element.964), channel_id=1, source_target_pairs={{1,0},{2,1},{3,2},{4,3},{5,4},{6,5},{7,6},{9,8},{10,9},{11,10},{12... | collective-permute-start | bytes 239624 | tf_op jit(solution)/shard_map/ppermute | solution.py:22
  134.9 18.9 %copy-start.3 = (pred[8]{0:T(512)(128)(4,1)S(1)}, pred[8]{0:T(512)(128)(4,1)}, u32[]{:S(2)}) copy-start(pred[8]{0:T(512)(128)(4,1)} %constant.296.clone.1) | copy-start | bytes 28
  135.0 5.0 %collective-permute-start.18 = (f32[3,3,14,128]{3,2,1,0:T(8,128)S(1)}, f32[3,3,14,128]{3,2,1,0:T(8,128)S(1)}, u32[]{:S(2)}, u32[]{:S(2)}) collective-permute-start(f32[3,3,14,128]{3,2,1,0:T(8,128)S(1)} %get-tuple-element.735), channel_id=1, source_target_pairs={{0,8},{8,16},{16,24},{1,9},{9,17},{17,25},{2,10},{10,18},{18,26},{... | collective-permute-start | bytes 193544 | tf_op jit(solution)/shard_map/ppermute | solution.py:21
  138.1 5.7 %collective-permute-start.19 = (f32[3,3,14,128]{3,2,1,0:T(8,128)S(1)}, f32[3,3,14,128]{3,2,1,0:T(8,128)S(1)}, u32[]{:S(2)}, u32[]{:S(2)}) collective-permute-start(f32[3,3,14,128]{3,2,1,0:T(8,128)S(1)} %get-tuple-element.736), channel_id=1, source_target_pairs={{8,0},{16,8},{24,16},{9,1},{17,9},{25,17},{10,2},{18,10},{26,18},{... | collective-permute-start | bytes 193544 | tf_op jit(solution)/shard_map/ppermute | solution.py:22
  143.8 7.4 %collective-permute-start.20 = (f32[3,20,3,128]{3,2,1,0:T(4,128)S(1)}, f32[3,20,3,128]{3,2,1,0:T(4,128)S(1)}, u32[]{:S(2)}, u32[]{:S(2)}) collective-permute-start(f32[3,20,3,128]{3,2,1,0:T(4,128)S(1)} %get-tuple-element.642), channel_id=1, source_target_pairs={{0,1},{1,2},{2,3},{3,4},{4,5},{5,6},{6,7},{8,9},{9,10},{10,11},{11... | collective-permute-start | bytes 276488 | tf_op jit(solution)/shard_map/ppermute | solution.py:21
  148.1 5.6 %collective-permute-start.21 = (f32[3,20,3,128]{3,2,1,0:T(4,128)S(1)}, f32[3,20,3,128]{3,2,1,0:T(4,128)S(1)}, u32[]{:S(2)}, u32[]{:S(2)}) collective-permute-start(f32[3,20,3,128]{3,2,1,0:T(4,128)S(1)} %get-tuple-element.643), channel_id=1, source_target_pairs={{1,0},{2,1},{3,2},{4,3},{5,4},{6,5},{7,6},{9,8},{10,9},{11,10},{12... | collective-permute-start | bytes 276488 | tf_op jit(solution)/shard_map/ppermute | solution.py:22
where the time goes:
time: 157 us; the launch traced here: 155 us
  starting transfers between devices  61.9 us (39%)
  waiting for transfers between devices  38.5 us (25%)
  other arithmetic  32.2 us (21%)
  local copies, waits for them, and re-layouts  18.9 us (12%)
  between operations  3.25 us (2%)
    ppermute x10, starting transfers between devices, extended_2(): before = lax.ppermute(last, axis, up)  30.8 us
    ppermute x10, starting transfers between devices, extended_2(): after = lax.ppermute(first, axis, down)  24.6 us
    ppermute x10, waiting for transfers between devices, extended_2(): after = lax.ppermute(first, axis, down)  23.9 us
    another operation x259, other arithmetic, force_partial(): jnp.stack([tension * component / length for component in components])  15 us
    slice x110, local copies, waits for them, and re-layouts, shift_depth(): return jnp.concatenate([values[..., offset:], zeros_block], -1)  13.2 us
    ppermute x10, waiting for transfers between devices, extended_2(): before = lax.ppermute(last, axis, up)  10.4 us
    ppermute x2, starting transfers between devices, passed_along(): return lax.ppermute(block, axis, route)  6.48 us
    add x2, other arithmetic, strain_partial(): own_sum = own_sum + contribution  4.22 us
  transfers between devices with their start and end apart: 22, of which 14 were waited for; matrix products, arithmetic and copies ran while one was open for 5% of the time, Pallas kernels for 0%

commit v1 on v0

v1 whole, which is shorter than its diff:
```python
import functools
import math

import jax
import jax.numpy as jnp
from jax import lax
from jax.experimental import pallas as pl
from jax.experimental.pallas import tpu as pltpu
from jax.sharding import PartitionSpec as P

STEPS = 2
TIME_STEP = 0.02
REACH = 3
MESH = pl.DeviceIdType.MESH
F32 = jnp.float32

AROUND = [(dx, dy) for dx in (-1, 0, 1) for dy in (-1, 0, 1) if (dx, dy) != (0, 0)]
SLOT = {direction: number for number, direction in enumerate(AROUND)}
STATE_TO = [(-1, 0), (0, -1), (0, 1), (-1, -1), (-1, 1)]
FINAL_TO = [(1, 0), (0, -1), (0, 1), (1, -1), (1, 1)]


def half_offsets():
    span = range(-REACH, REACH + 1)
    return [
        (a, b, c)
        for a in span
        for b in span
        for c in span
        if a * a + b * b + c * c <= REACH * REACH and (a, b, c) > (0, 0, 0)
    ]


OFFSETS = half_offsets()
GROUPS = {}
for _k, (_a, _b, _c) in enumerate(OFFSETS):
    GROUPS.setdefault((_a, _b), []).append((_k, _c))
RADII = [math.sqrt(float(a * a + b * b + c * c)) for a, b, c in OFFSETS]
VOLUME = 2.0 * sum(RADII)


def round_up(value, unit):
    return -(-value // unit) * unit


def tree_sum(terms):
    while len(terms) > 1:
        terms = [
            terms[n] + terms[n + 1] if n + 1 < len(terms) else terms[n]
            for n in range(0, len(terms), 2)
        ]
    return terms[0]


def kernel(
    grid_rows,
    grid_cols,
    u_ref,
    v_ref,
    intact_hbm,
    mat_ref,
    bulk_ref,
    shear_ref,
    dens_ref,
    out_u,
    out_v,
    out_f,
    intact_ref,
    flag,
    wide_u,
    wide_v,
    u_shift,
    a_shift,
    b_shift,
    a_coef,
    inertia,
    strain,
    force,
    vm,
    pack_u,
    pack_vm,
    pack_t,
    pack_f,
    u_x,
    u_y,
    u_d,
    vm_x,
    vm_y,
    vm_d,
    t_x,
    t_y,
    t_d,
    f_x,
    f_y,
    f_d,
    local_sem,
    send_sem,
    recv_sem,
):
    rows, cols, nz = mat_ref.shape
    wide_rows = rows + REACH
    padded = wide_u.shape[2]
    gx = lax.axis_index("gx")
    gy = lax.axis_index("gy")

    def present(direction):
        x = gx + direction[0]
        y = gy + direction[1]
        return (x >= 0) & (x < grid_rows) & (y >= 0) & (y < grid_cols)

    here = {direction: present(direction) for direction in AROUND}

    load = pltpu.make_async_copy(intact_hbm, intact_ref, local_sem)
    load.start()

    barrier = pltpu.get_barrier_semaphore()
    for direction in AROUND:

        @pl.when(here[direction])
        def _(direction=direction):
            pl.semaphore_signal(
                barrier,
                inc=1,
                device_id=(gx + direction[0], gy + direction[1]),
                device_id_type=MESH,
            )

    for comp in range(3):
        for r in range(rows):
            pack_u[0, comp, 3 * r : 3 * r + 3] = u_ref[comp, r, 0:3]
            pack_u[1, comp, 3 * r : 3 * r + 3] = u_ref[comp, r, cols - 3 : cols]
    vm[0:3] = v_ref[...]
    vm[3] = mat_ref[...].astype(F32)
    for comp in range(4):
        for r in range(rows):
            pack_vm[0, comp, 3 * r : 3 * r + 3] = vm[comp, r, 0:3]
            pack_vm[1, comp, 3 * r : 3 * r + 3] = vm[comp, r, cols - 3 : cols]

    on_x = (gx > 0).astype(jnp.int32) + (gx < grid_rows - 1).astype(jnp.int32)
    on_y = (gy > 0).astype(jnp.int32) + (gy < grid_cols - 1).astype(jnp.int32)
    pl.semaphore_wait(barrier, (1 + on_x) * (1 + on_y) - 1)

    def copy_to(stage, direction, source, target):
        opposite = SLOT[(-direction[0], -direction[1])]
        return pltpu.make_async_remote_copy(
            src_ref=source,
            dst_ref=target,
            send_sem=send_sem.at[stage, SLOT[direction]],
            recv_sem=recv_sem.at[stage, opposite],
            device_id=(gx + direction[0], gy + direction[1]),
            device_id_type=MESH,
        )

    def side(value):
        return 0 if value < 0 else 1

    def state_source(direction, whole, pack):
        dx, dy = direction
        if dy == 0:
            return whole.at[:, 0:REACH]
        if dx == 0:
            return pack.at[side(dy)]
        return pack.at[side(dy), :, 0:16]

    def state_target(origin, x_buf, y_buf, d_buf):
        dx, dy = origin
        if dy == 0:
            return x_buf
        if dx == 0:
            return y_buf.at[side(dy)]
        return d_buf.at[side(dy)]

    def sum_source(direction, whole, pack, final):
        dx, dy = direction
        first = rows if dx > 0 else 0
        lead = (slice(None),)
        if dy == 0:
            return whole.at[lead + (slice(first, first + REACH),)]
        if dx == 0:
            if final:
                return pack.at[(side(dy),) + lead + (slice(0, 6 * rows),)]
            return pack.at[side(dy)]
        return pack.at[(side(dy),) + lead + (slice(6 * first, 6 * first + 24),)]

    def sum_target(origin, x_buf, y_buf, d_buf, step, final):
        dx, dy = origin
        lead = (slice(None),)
        if dy == 0:
            return x_buf.at[step, side(dx)]
        if dx == 0:
            if final:
                return y_buf.at[(step, side(dy)) + lead + (slice(0, 6 * rows),)]
            return y_buf.at[step, side(dy)]
        return d_buf.at[step, 2 * side(dx) + side(dy)]

    def start_all(stage, receivers, source_of, target_of):
        for direction in receivers:

            @pl.when(here[direction])
            def _(direction=direction):
                origin = (-direction[0], -direction[1])
                copy_to(stage, direction, source_of(direction), target_of(origin)).start()

    def wait_recv(stage, direction, source_of, target_of):
        origin = (-direction[0], -direction[1])
        target = target_of(origin)
        pltpu.make_async_remote_copy(
            src_ref=target,
            dst_ref=target,
            send_sem=send_sem.at[stage, SLOT[direction]],
            recv_sem=recv_sem.at[stage, SLOT[origin]],
            device_id=(gx + origin[0], gy + origin[1]),
            device_id_type=MESH,
        ).wait_recv()

    def wait_sends(stage, receivers, source_of, target_of):
        for direction in receivers:

            @pl.when(here[direction])
            def _(direction=direction):
                origin = (-direction[0], -direction[1])
                copy_to(stage, direction, source_of(direction), target_of(origin)).wait_send()

    u_plan = (
        lambda d: state_source(d, u_ref, pack_u),
        lambda o: state_target(o, u_x, u_y, u_d),
    )
    vm_plan = (
        lambda d: state_source(d, vm, pack_vm),
        lambda o: state_target(o, vm_x, vm_y, vm_d),
    )
    start_all(0, STATE_TO, *u_plan)
    start_all(1, STATE_TO, *vm_plan)

    lane = lax.broadcasted_iota(jnp.int32, (padded, nz), 1)

    def shifted(values, c):
        if c == 0:
            return values
        moved = pltpu.roll(values, (-c) % nz, axis=1)
        return jnp.where((lane + c >= 0) & (lane + c < nz), moved, 0.0)

    def take_state(stage, plan, wide_of, comps):
        for direction in STATE_TO:
            origin = (-direction[0], -direction[1])

            @pl.when(here[origin])
            def _(direction=direction, origin=origin):
                wait_recv(stage, direction, *plan)
                dx, dy = origin
                buf = plan[1](origin)
                for comp in range(comps):
                    wide = wide_of(comp)
                    if dy == 0:
                        for r in range(REACH):
                            wide[rows + r, REACH : REACH + cols] = buf[comp, r]
                        continue
                    at = 0 if dy < 0 else REACH + cols
                    for r in range(rows if dx == 0 else REACH):
                        row = r if dx == 0 else rows + r
                        wide[row, at : at + REACH] = buf[comp, 3 * r : 3 * r + 3]

        wait_sends(stage, STATE_TO, *plan)

    wide_u[...] = jnp.zeros(wide_u.shape, F32)
    wide_v[...] = jnp.zeros(wide_v.shape, F32)
    for comp in range(3):
        wide_u[comp, 0:rows, REACH : REACH + cols] = u_ref[comp]
    for comp in range(4):
        wide_v[comp, 0:rows, REACH : REACH + cols] = vm[comp]

    def shift_motion():
        @pl.loop(0, wide_rows)
        def _(r):
            for comp in range(3):
                values = wide_u[comp, r]
                for c in range(-REACH, REACH + 1):
                    moved = shifted(values, c)
                    if comp == 2 and c != 0:
                        moved = moved + float(c)
                    u_shift[c + REACH, comp, r] = moved

    def materials():
        @pl.loop(0, wide_rows)
        def _(r):
            classes = wide_v[3, r]
            bulk = jnp.full(classes.shape, bulk_ref[0], F32)
            shear = jnp.full(classes.shape, shear_ref[0], F32)
            dens = jnp.full(classes.shape, dens_ref[0], F32)
            for number in range(1, bulk_ref.shape[0]):
                match = classes == float(number)
                bulk = jnp.where(match, bulk_ref[number], bulk)
                shear = jnp.where(match, shear_ref[number], shear)
                dens = jnp.where(match, dens_ref[number], dens)
            inertia[r] = TIME_STEP / dens
            a_coef[r] = (9.0 / (VOLUME * VOLUME)) * (bulk - (5.0 / 3.0) * shear)
            stiff = (15.0 / VOLUME) * shear
            for c in range(-REACH, REACH + 1):
                b_shift[c + REACH, r] = shifted(stiff, c)

    depth = lax.broadcasted_iota(jnp.int32, (cols, nz), 1)
    column = lax.broadcasted_iota(jnp.int32, (cols, nz), 0) + gy * cols

    def geometry(i, a, b, c, own):
        at = pl.ds(REACH + b, cols)
        y0 = u_shift[c + REACH, 0, i + a, at] - own[0][a]
        y1 = u_shift[c + REACH, 1, i + a, at] - own[1][b]
        y2 = u_shift[c + REACH, 2, i + a, at] - own[2]
        square = y0 * y0 + y1 * y1 + y2 * y2
        inverse = lax.rsqrt(square)
        return (y0, y1, y2), square * inverse, inverse

    def own_motion(i):
        mine = [wide_u[comp, i, REACH : REACH + cols] for comp in range(3)]
        by_row = {a: mine[0] - float(a) for a in range(REACH + 1)}
        by_col = {b: mine[1] - float(b) for b in range(-REACH, REACH + 1)}
        return (by_row, by_col, mine[2])

    def back(values, c):
        return values if c == 0 else pltpu.roll(values, c % nz, axis=1)

    def strain_pass(first):
        strain[...] = jnp.zeros(strain.shape, F32)

        @pl.loop(0, rows)
        def _(i):
            own = own_motion(i)
            if first:
                lane_in = {
                    c: jnp.where((depth + c >= 0) & (depth + c < nz), 1.0, 0.0)
                    for c in range(-REACH, REACH + 1)
                }
            sums = []
            for (a, b), members in GROUPS.items():
                if first:
                    row_in = (gx * rows + i + a) < grid_rows * rows
                    plane = jnp.where(
                        (column + b >= 0) & (column + b < grid_cols * cols) & row_in, 1.0, 0.0
                    )
                returned = []
                for k, c in members:
                    _, length, _ = geometry(i, a, b, c, own)
                    if first:
                        weight = intact_ref[k, i].astype(F32) * (plane * lane_in[c])
                        flag[k, i] = weight
                    else:
                        weight = flag[k, i]
                    term = weight * (length - RADII[k])
                    sums.append(term)
                    returned.append(back(term, c))
                at = pl.ds(REACH + b, cols)
                strain[0, i + a, at] = strain[0, i + a, at] + tree_sum(returned)
                sums = [tree_sum(sums)]
            at = pl.ds(REACH, cols)
            strain[0, i, at] = strain[0, i, at] + sums[0]

    def force_pass():
        force[...] = jnp.zeros(force.shape, F32)

        @pl.loop(0, rows)
        def _(i):
            own = own_motion(i)
            mid = pl.ds(REACH, cols)
            own_a = a_shift[REACH, i, mid]
            own_b = b_shift[REACH, i, mid]
            sums = [[], [], []]
            for (a, b), members in GROUPS.items():
                at = pl.ds(REACH + b, cols)
                returned = [[], [], []]
                for k, c in members:
                    y, length, inverse = geometry(i, a, b, c, own)
                    both_a = own_a + a_shift[c + REACH, i + a, at]
                    both_b = own_b + b_shift[c + REACH, i + a, at]
                    relative = (length - RADII[k]) * (1.0 / RADII[k])
                    tension = flag[k, i] * (both_a + both_b * relative) * inverse
                    for comp in range(3):
                        term = tension * y[comp]
                        sums[comp].append(term)
                        returned[comp].append(back(term, c))
                for comp in range(3):
                    force[comp, i + a, at] = force[comp, i + a, at] - tree_sum(returned[comp])
                    sums[comp] = [tree_sum(sums[comp])]
            for comp in range(3):
                force[comp, i, mid] = force[comp, i, mid] + sums[comp][0]

    def pack_sums(whole, pack, last_row):
        for comp in range(whole.shape[0]):
            for r in range(last_row):
                pack[0, comp, 6 * r : 6 * r + 6] = whole[comp, r, 0:6]
                pack[1, comp, 6 * r : 6 * r + 6] = whole[comp, r, cols : cols + 6]

    def take_sums(stage, senders, plan, whole, comps, final):
        wait_sends(stage, senders, *plan)
        for direction in senders:
            origin = (-direction[0], -direction[1])

            @pl.when(here[origin])
            def _(direction=direction, origin=origin):
                wait_recv(stage, direction, *plan)
                dx, dy = origin
                buf = plan[1](origin)
                for comp in range(comps):
                    if dy == 0:
                        first = 0 if dx < 0 else rows
                        for r in range(REACH):
                            whole[comp, first + r] = whole[comp, first + r] + buf[comp, r]
                        continue
                    at = pl.ds(0 if dy < 0 else cols, 6)
                    if dx == 0:
                        span = [(r, r) for r in range(rows if final else wide_rows)]
                    else:
                        span = [(r, r + (0 if dx < 0 else rows)) for r in range(REACH)]
                    for r, row in span:
                        whole[comp, row, at] = whole[comp, row, at] + buf[comp, 6 * r : 6 * r + 6]

    take_state(0, u_plan, lambda comp: wide_u.at[comp], 3)
    shift_motion()
    load.wait()

    for step in range(STEPS):
        last = step == STEPS - 1
        strain_pass(step == 0)
        pack_sums(strain, pack_t, wide_rows)
        t_plan = (
            lambda d: sum_source(d, strain, pack_t, False),
            lambda o, step=step: sum_target(o, t_x, t_y, t_d, step, False),
        )
        start_all(2 + 2 * step, AROUND, *t_plan)
        if step == 0:
            take_state(1, vm_plan, lambda comp: wide_v.at[comp], 4)
            materials()
        take_sums(2 + 2 * step, AROUND, t_plan, strain, 1, False)

        @pl.loop(0, wide_rows)
        def _(r):
            values = strain[0, r] * a_coef[r]
            for c in range(-REACH, REACH + 1):
                a_shift[c + REACH, r] = shifted(values, c)

        force_pass()
        pack_sums(force, pack_f, wide_rows)
        receivers = FINAL_TO if last else AROUND
        f_plan = (
            lambda d, last=last: sum_source(d, force, pack_f, last),
            lambda o, step=step, last=last: sum_target(o, f_x, f_y, f_d, step, last),
        )
        start_all(3 + 2 * step, receivers, *f_plan)
        take_sums(3 + 2 * step, receivers, f_plan, force, 3, last)
        if not last:

            @pl.loop(0, wide_rows)
            def _(r):
                for comp in range(3):
                    speed = wide_v[comp, r] + force[comp, r] * inertia[r]
                    wide_v[comp, r] = speed
                    wide_u[comp, r] = wide_u[comp, r] + TIME_STEP * speed

            shift_motion()
        else:
            mid = pl.ds(REACH, cols)

            @pl.loop(0, rows)
            def _(r):
                for comp in range(3):
                    pull = force[comp, r, mid]
                    speed = wide_v[comp, r, mid] + pull * inertia[r, mid]
                    out_f[comp, r] = pull
                    out_v[comp, r] = speed
                    out_u[comp, r] = wide_u[comp, r, mid] + TIME_STEP * speed


def on_device(displacement, velocity, intact, material, bulk_modulus, shear_modulus, density):
    rows, cols, nz = material.shape
    wide_rows = rows + REACH
    padded = round_up(cols + 2 * REACH, 8)
    packed = round_up(6 * wide_rows, 8)
    own = jax.ShapeDtypeStruct((3, rows, cols, nz), F32)
    vmem = pl.BlockSpec(memory_space=pltpu.VMEM)
    smem = pl.BlockSpec(memory_space=pltpu.SMEM)
    stages = 2 + 2 * STEPS

    def buffer(*shape):
        return pltpu.VMEM(shape + (nz,), F32)

    return pl.pallas_call(
        functools.partial(kernel, lax.axis_size("gx"), lax.axis_size("gy")),
        out_shape=(own, own, own),
        in_specs=[vmem, vmem, pl.BlockSpec(memory_space=pl.ANY), vmem, smem, smem, smem],
        out_specs=(vmem, vmem, vmem),
        scratch_shapes=[
            pltpu.VMEM(intact.shape, jnp.int32),
            pltpu.VMEM(intact.shape, F32),
            buffer(3, wide_rows, padded),
            buffer(4, wide_rows, padded),
            buffer(7, 3, wide_rows, padded),
            buffer(7, wide_rows, padded),
            buffer(7, wide_rows, padded),
            buffer(wide_rows, padded),
            buffer(wide_rows, padded),
            buffer(1, wide_rows, padded),
            buffer(3, wide_rows, padded),
            buffer(4, rows, cols),
            buffer(2, 3, 3 * rows),
            buffer(2, 4, 3 * rows),
            buffer(2, 1, packed),
            buffer(2, 3, packed),
            buffer(3, REACH, cols),
            buffer(2, 3, 3 * rows),
            buffer(2, 3, 16),
            buffer(4, REACH, cols),
            buffer(2, 4, 3 * rows),
            buffer(2, 4, 16),
            buffer(STEPS, 2, 1, REACH, padded),
            buffer(STEPS, 2, 1, packed),
            buffer(STEPS, 4, 1, 24),
            buffer(STEPS, 2, 3, REACH, padded),
            buffer(STEPS, 2, 3, packed),
            buffer(STEPS, 4, 3, 24),
            pltpu.SemaphoreType.DMA,
            pltpu.SemaphoreType.DMA((stages, 8)),
            pltpu.SemaphoreType.DMA((stages, 8)),
        ],
        compiler_params=pltpu.CompilerParams(
            collective_id=0, has_side_effects=True, vmem_limit_bytes=48 * 1024 * 1024
        ),
        name="peridynamics",
    )(displacement, velocity, intact, material, bulk_modulus, shear_modulus, density)


def solution(mesh):
    node = P(None, "gx", "gy", None)
    return jax.shard_map(
        on_device,
        mesh=mesh,
        in_specs=(node, node, node, P("gx", "gy", None), P(), P(), P()),
        out_specs=(node, node, node),
        check_vma=False,
    )
```

time: 157 us -> 55.1 us (0.35); the launches traced: 155 us -> 54.8 us
  starting transfers between devices: 61.9 us -> 0 us
  Pallas kernels: 0 us -> 46.2 us
  waiting for transfers between devices: 38.5 us -> 0 us
  other arithmetic: 32.2 us -> 0 us
  local copies, waits for them, and re-layouts: 18.9 us -> 7.98 us
  between operations: 3.25 us -> 0.66 us
    ppermute x22 -> x0, starting transfers between devices: 61.9 us -> none  [the longest x10 30.8 us: extended_2(): before = lax.ppermute(last, axis, up)]
    pallas_call x0 -> x1, Pallas kernels: none -> 46.2 us  [on_device(): pl.pallas_call(functools.partial(kernel, lax.axis_size('gx'), lax.axis_si...]
    ppermute x22 -> x0, waiting for transfers between devices: 38.5 us -> none  [the longest x10 23.9 us: extended_2(): after = lax.ppermute(first, axis, down)]
    slice x139 -> x0, local copies, waits for them, and re-layouts: 15.8 us -> none  [the longest x110 13.2 us: shift_depth(): return jnp.concatenate([values[..., offset:], zeros_block], -1)]
    another operation x259 -> x0, other arithmetic: 15 us -> none  [force_partial(): jnp.stack([tension * component / length for component in components])]
    add x14 -> x0, other arithmetic: 11.6 us -> none  [the longest x2 4.22 us: strain_partial(): own_sum = own_sum + contribution]
    unnamed x9 -> x17, local copies, waits for them, and re-layouts: 2.2 us -> 7.98 us
    concatenate x14 -> x0, other arithmetic: 2.65 us -> none  [the longest x11 1.61 us: extended_2(): shard = jnp.concatenate([before, shard, after], axis=dim)]
  transfers between devices with their start and end apart: 22 -> 0, of which waited for: 14 -> 0; matrix products, arithmetic and copies ran while one was open for 5% -> 0% of each run, Pallas kernels for 0% -> 0%
where the time goes in v1:
time: 55.1 us; the launch traced here: 54.8 us
  Pallas kernels  46.2 us (84%)
  local copies, waits for them, and re-layouts  7.98 us (14%)
  between operations  0.66 us (1%)
    pallas_call x1, Pallas kernels, on_device(): pl.pallas_call(functools.partial(kernel, lax.axis_size('gx'), lax.axis_si...  46.2 us
    unnamed x17, local copies, waits for them, and re-layouts  7.98 us

profile of v1, /device:TPU:9, one launch (start us, length us, event | category | flops | bytes accessed | tf_op | source)
XLA Modules:
  0.0 54.8 jit_solution(1064236214584739340)
XLA Ops:
  0.6 0.0 copy-start
  0.6 1.5 %copy-done = s32[61,8,8,128]{3,2,1,0:T(8,128)S(1)} copy-done((s32[61,8,8,128]{3,2,1,0:T(8,128)S(1)}, s32[61,8,8,128]{3,2,1,0:T(8,128)}, u32[]{:S(2)}) %copy-start) | copy-done | bytes 1998872
  2.2 0.0 copy-start.1
  2.2 0.9 %copy-done.1 = f32[3,8,8,128]{3,2,1,0:T(8,128)S(1)} copy-done((f32[3,8,8,128]{3,2,1,0:T(8,128)S(1)}, f32[3,8,8,128]{3,2,1,0:T(8,128)}, u32[]{:S(2)}) %copy-start.1) | copy-done | bytes 98328
  3.1 0.0 copy-start.2
  3.1 0.9 %copy-done.2 = f32[3,8,8,128]{3,2,1,0:T(8,128)S(1)} copy-done((f32[3,8,8,128]{3,2,1,0:T(8,128)S(1)}, f32[3,8,8,128]{3,2,1,0:T(8,128)}, u32[]{:S(2)}) %copy-start.2) | copy-done | bytes 98328
  4.0 0.0 copy-start.3
  4.0 0.8 %copy-done.3 = s32[8,8,128]{2,1,0:T(8,128)S(1)} copy-done((s32[8,8,128]{2,1,0:T(8,128)S(1)}, s32[8,8,128]{2,1,0:T(8,128)}, u32[]{:S(2)}) %copy-start.3) | copy-done | bytes 32792
  4.7 0.0 copy-start.4
  4.7 0.7 %copy-done.4 = f32[8]{0:T(128)S(1)} copy-done((f32[8]{0:T(128)S(1)}, f32[8]{0:T(128)}, u32[]{:S(2)}) %copy-start.4) | copy-done | bytes 56
  5.4 0.0 copy-start.5
  5.4 0.7 %copy-done.5 = f32[8]{0:T(128)S(1)} copy-done((f32[8]{0:T(128)S(1)}, f32[8]{0:T(128)}, u32[]{:S(2)}) %copy-start.5) | copy-done | bytes 56
  6.0 0.0 copy-start.6
  6.0 0.7 %copy-done.6 = f32[8]{0:T(128)S(1)} copy-done((f32[8]{0:T(128)S(1)}, f32[8]{0:T(128)}, u32[]{:S(2)}) %copy-start.6) | copy-done | bytes 56
  6.7 46.2 %peridynamics.1 = (f32[3,8,8,128]{3,2,1,0:T(8,128)S(1)}, f32[3,8,8,128]{3,2,1,0:T(8,128)S(1)}, f32[3,8,8,128]{3,2,1,0:T(8,128)S(1)}) custom-call(f32[3,8,8,128]{3,2,1,0:T(8,128)S(1)} %copy-done.1, f32[3,8,8,128]{3,2,1,0:T(8,128)S(1)} %copy-done.2, s32[61,8,8,128]{3,2,1,0:T(8,128)S(1)} %copy-done, s32[8,8,128]{2,1,0:T(8,128)S(1)} %copy-done.3, ...), custom_call_target="tpu_custom_call" | custom-call | tf_op jit(solution)/shard_map/peridynamics/pallas_call | solution.py:485
  52.9 0.6 %copy.13 = f32[3,8,8,128]{3,2,1,0:T(8,128)} copy(f32[3,8,8,128]{3,2,1,0:T(8,128)S(1)} %get-tuple-element.6) | data formatting | bytes 196608
  53.5 0.6 %copy.14 = f32[3,8,8,128]{3,2,1,0:T(8,128)} copy(f32[3,8,8,128]{3,2,1,0:T(8,128)S(1)} %get-tuple-element.7) | data formatting | bytes 196608
  54.2 0.6 %copy.15 = f32[3,8,8,128]{3,2,1,0:T(8,128)} copy(f32[3,8,8,128]{3,2,1,0:T(8,128)S(1)} %get-tuple-element.8) | data formatting | bytes 196608
Async XLA Ops:
  0.6 1.6 %copy-start = (s32[61,8,8,128]{3,2,1,0:T(8,128)S(1)}, s32[61,8,8,128]{3,2,1,0:T(8,128)}, u32[]{:S(2)}) copy-start(s32[61,8,8,128]{3,2,1,0:T(8,128)} %intact_hbm.1) | copy-start | bytes 5996548
  2.2 0.9 %copy-start.1 = (f32[3,8,8,128]{3,2,1,0:T(8,128)S(1)}, f32[3,8,8,128]{3,2,1,0:T(8,128)}, u32[]{:S(2)}) copy-start(f32[3,8,8,128]{3,2,1,0:T(8,128)} %u_ref.1) | copy-start | bytes 294916
  3.1 0.9 %copy-start.2 = (f32[3,8,8,128]{3,2,1,0:T(8,128)S(1)}, f32[3,8,8,128]{3,2,1,0:T(8,128)}, u32[]{:S(2)}) copy-start(f32[3,8,8,128]{3,2,1,0:T(8,128)} %v_ref.1) | copy-start | bytes 294916
  4.0 0.8 %copy-start.3 = (s32[8,8,128]{2,1,0:T(8,128)S(1)}, s32[8,8,128]{2,1,0:T(8,128)}, u32[]{:S(2)}) copy-start(s32[8,8,128]{2,1,0:T(8,128)} %mat_ref.1) | copy-start | bytes 98308
  4.7 0.7 %copy-start.4 = (f32[8]{0:T(128)S(1)}, f32[8]{0:T(128)}, u32[]{:S(2)}) copy-start(f32[8]{0:T(128)} %bulk_ref.1) | copy-start | bytes 100
  5.4 0.7 %copy-start.5 = (f32[8]{0:T(128)S(1)}, f32[8]{0:T(128)}, u32[]{:S(2)}) copy-start(f32[8]{0:T(128)} %shear_ref.1) | copy-start | bytes 100
  6.0 0.7 %copy-start.6 = (f32[8]{0:T(128)S(1)}, f32[8]{0:T(128)}, u32[]{:S(2)}) copy-start(f32[8]{0:T(128)} %dens_ref.1) | copy-start | bytes 100

commit v2 on v1

v2 whole, which is shorter than its diff:
```python
import functools
import math

import jax
import jax.numpy as jnp
from jax import lax
from jax.experimental import pallas as pl
from jax.experimental.pallas import tpu as pltpu
from jax.sharding import PartitionSpec as P

STEPS = 2
TIME_STEP = 0.02
REACH = 3
NEAR = 2
MESH = pl.DeviceIdType.MESH
F32 = jnp.float32

AROUND = [(dx, dy) for dx in (-1, 0, 1) for dy in (-1, 0, 1) if (dx, dy) != (0, 0)]
STATE = [("S", (-1, 0)), ("S", (0, -1)), ("S", (0, 1)), ("S", (-1, -1)), ("S", (-1, 1))]
CHUNKS = {
    "C": [("C", (1, 0)), ("C", (1, -1)), ("C", (1, 1)), ("C", (0, -1)), ("C", (0, 1))],
    "A": [("A", (-1, 0)), ("A", (-1, -1)), ("A", (-1, 1)), ("A", (0, -1)), ("A", (0, 1))],
    "B": [("B", (0, -1)), ("B", (0, 1))],
}
FINAL = {
    "C": [("C", (1, 0)), ("C", (1, -1)), ("C", (1, 1))],
    "A": [("A", (0, -1)), ("A", (0, 1))],
    "B": [("B", (0, -1)), ("B", (0, 1))],
}
SLOT = {key: n for n, key in enumerate(CHUNKS["C"] + CHUNKS["A"] + CHUNKS["B"])}
SLOT.update({key: n for n, key in enumerate(STATE)})


def half_offsets():
    span = range(-REACH, REACH + 1)
    return [
        (a, b, c)
        for a in span
        for b in span
        for c in span
        if a * a + b * b + c * c <= REACH * REACH and (a, b, c) > (0, 0, 0)
    ]


OFFSETS = half_offsets()
GROUPS = {}
for _k, (_a, _b, _c) in enumerate(OFFSETS):
    GROUPS.setdefault((_a, _b), []).append((_k, _c))
RADII = [math.sqrt(float(a * a + b * b + c * c)) for a, b, c in OFFSETS]
VOLUME = 2.0 * sum(RADII)


def round_up(value, unit):
    return -(-value // unit) * unit


def tree_sum(terms):
    while len(terms) > 1:
        terms = [
            terms[n] + terms[n + 1] if n + 1 < len(terms) else terms[n]
            for n in range(0, len(terms), 2)
        ]
    return terms[0]


def kernel(
    grid_rows,
    grid_cols,
    u_hbm,
    v_hbm,
    intact_hbm,
    mat_hbm,
    bulk_hbm,
    shear_hbm,
    dens_hbm,
    out_u,
    out_v,
    out_f,
    u_ref,
    mat_ref,
    bulk_ref,
    shear_ref,
    dens_ref,
    intact_ref,
    flag,
    by_inverse,
    by_stretch,
    wide_u,
    wide_v,
    u_shift,
    a_shift,
    b_shift,
    a_coef,
    inertia,
    strain,
    force,
    vm,
    pack_u,
    pack_vm,
    pack_t,
    pack_f,
    u_x,
    u_y,
    u_d,
    vm_x,
    vm_y,
    vm_d,
    t_x,
    t_y,
    t_d,
    f_x,
    f_y,
    f_d,
    local_sem,
    send_sem,
    recv_sem,
):
    rows, cols, nz = mat_ref.shape
    wide_rows = rows + REACH
    padded = wide_u.shape[2]
    gx = lax.axis_index("gx")
    gy = lax.axis_index("gy")

    def present(direction):
        x = gx + direction[0]
        y = gy + direction[1]
        return (x >= 0) & (x < grid_rows) & (y >= 0) & (y < grid_cols)

    here = {direction: present(direction) for direction in AROUND}

    barrier = pltpu.get_barrier_semaphore()
    for direction in AROUND:

        @pl.when(here[direction])
        def _(direction=direction):
            pl.semaphore_signal(
                barrier,
                inc=1,
                device_id=(gx + direction[0], gy + direction[1]),
                device_id_type=MESH,
            )

    loads = [
        pltpu.make_async_copy(source, target, local_sem.at[n])
        for n, (source, target) in enumerate(
            [
                (u_hbm, u_ref),
                (v_hbm, vm.at[0:3]),
                (mat_hbm, mat_ref),
                (intact_hbm, intact_ref),
                (bulk_hbm, bulk_ref),
                (shear_hbm, shear_ref),
                (dens_hbm, dens_ref),
            ]
        )
    ]
    for load in loads:
        load.start()

    loads[0].wait()
    for comp in range(3):
        for r in range(rows):
            pack_u[0, comp, 3 * r : 3 * r + 3] = u_ref[comp, r, 0:3]
            pack_u[1, comp, 3 * r : 3 * r + 3] = u_ref[comp, r, cols - 3 : cols]

    on_x = (gx > 0).astype(jnp.int32) + (gx < grid_rows - 1).astype(jnp.int32)
    on_y = (gy > 0).astype(jnp.int32) + (gy < grid_cols - 1).astype(jnp.int32)
    pl.semaphore_wait(barrier, (1 + on_x) * (1 + on_y) - 1)

    def copy_to(stage, key, source, target):
        dx, dy = key[1]
        return pltpu.make_async_remote_copy(
            src_ref=source,
            dst_ref=target,
            send_sem=send_sem.at[stage, SLOT[key]],
            recv_sem=recv_sem.at[stage, SLOT[key]],
            device_id=(gx + dx, gy + dy),
            device_id_type=MESH,
        )

    def side(value):
        return 0 if value < 0 else 1

    def state_source(key, whole, pack):
        dx, dy = key[1]
        if dy == 0:
            return whole.at[:, 0:REACH]
        if dx == 0:
            return pack.at[side(dy)]
        return pack.at[side(dy), :, 0:16]

    def state_target(key, x_buf, y_buf, d_buf):
        dx, dy = key[1]
        if dy == 0:
            return x_buf
        if dx == 0:
            return y_buf.at[side(-dy)]
        return d_buf.at[side(-dy)]

    rows_of = {"A": (0, REACH), "B": (REACH, rows), "C": (rows, wide_rows)}
    wide_a = round_up(6 * REACH, 8)
    wide_b = round_up(6 * (rows - REACH), 8)
    start_of = {"A": 0, "B": wide_a, "C": wide_a + wide_b}

    def packed_rows(chunk, final):
        first, end = rows_of[chunk]
        start = start_of[chunk]
        return slice(start, start + round_up((3 if final else 6) * (end - first), 8))

    def sum_source(key, whole, pack, final):
        chunk, (dx, dy) = key
        if dy == 0:
            return whole.at[:, slice(*rows_of[chunk])]
        return pack.at[side(dy), :, packed_rows(chunk, final)]

    def sum_target(key, x_buf, y_buf, d_buf, step, final):
        chunk, (dx, dy) = key
        if dy == 0:
            return x_buf.at[step, side(-dx)]
        span = packed_rows(chunk, final)
        if dx == 0:
            return y_buf.at[step, side(-dy), :, span]
        return d_buf.at[step, 2 * side(-dx) + side(-dy), :, 0 : span.stop - span.start]

    def start_all(stage, keys, source_of, target_of):
        for key in keys:

            @pl.when(here[key[1]])
            def _(key=key):
                copy_to(stage, key, source_of(key), target_of(key)).start()

    def wait_recv(stage, key, source_of, target_of):
        target = target_of(key)
        pltpu.make_async_remote_copy(
            src_ref=target,
            dst_ref=target,
            send_sem=send_sem.at[stage, SLOT[key]],
            recv_sem=recv_sem.at[stage, SLOT[key]],
            device_id=(gx - key[1][0], gy - key[1][1]),
            device_id_type=MESH,
        ).wait_recv()

    def wait_sends(stage, keys, source_of, target_of):
        for key in keys:

            @pl.when(here[key[1]])
            def _(key=key):
                copy_to(stage, key, source_of(key), target_of(key)).wait_send()

    u_plan = (
        lambda d: state_source(d, u_ref, pack_u),
        lambda o: state_target(o, u_x, u_y, u_d),
    )
    vm_plan = (
        lambda d: state_source(d, vm, pack_vm),
        lambda o: state_target(o, vm_x, vm_y, vm_d),
    )
    start_all(0, STATE, *u_plan)
    loads[1].wait()
    loads[2].wait()
    vm[3] = mat_ref[...].astype(F32)
    for comp in range(4):
        for r in range(rows):
            pack_vm[0, comp, 3 * r : 3 * r + 3] = vm[comp, r, 0:3]
            pack_vm[1, comp, 3 * r : 3 * r + 3] = vm[comp, r, cols - 3 : cols]
    start_all(1, STATE, *vm_plan)

    def shifted(values, c):
        if c == 0:
            return values
        lane = lax.broadcasted_iota(jnp.int32, values.shape, 1)
        moved = pltpu.roll(values, (-c) % nz, axis=1)
        return jnp.where((lane + c >= 0) & (lane + c < nz), moved, 0.0)

    def take_state(stage, plan, wide_of, comps):
        for key in STATE:
            origin = (-key[1][0], -key[1][1])

            @pl.when(here[origin])
            def _(key=key, origin=origin):
                wait_recv(stage, key, *plan)
                dx, dy = origin
                buf = plan[1](key)
                for comp in range(comps):
                    wide = wide_of(comp)
                    if dy == 0:
                        for r in range(REACH):
                            wide[rows + r, REACH : REACH + cols] = buf[comp, r]
                        continue
                    at = 0 if dy < 0 else REACH + cols
                    for r in range(rows if dx == 0 else REACH):
                        row = r if dx == 0 else rows + r
                        wide[row, at : at + REACH] = buf[comp, 3 * r : 3 * r + 3]


    wide_u[...] = jnp.zeros(wide_u.shape, F32)
    wide_v[...] = jnp.zeros(wide_v.shape, F32)
    for comp in range(3):
        wide_u[comp, 0:rows, REACH : REACH + cols] = u_ref[comp]
    for comp in range(4):
        wide_v[comp, 0:rows, REACH : REACH + cols] = vm[comp]

    def shift_motion():
        @pl.loop(0, wide_rows)
        def _(r):
            for comp in range(3):
                values = wide_u[comp, r]
                for c in range(-NEAR, NEAR + 1):
                    moved = shifted(values, c)
                    if comp == 2 and c != 0:
                        moved = moved + float(c)
                    u_shift[c + NEAR, comp, r] = moved

    def materials():
        @pl.loop(0, wide_rows)
        def _(r):
            classes = wide_v[3, r]
            bulk = jnp.full(classes.shape, bulk_ref[0], F32)
            shear = jnp.full(classes.shape, shear_ref[0], F32)
            dens = jnp.full(classes.shape, dens_ref[0], F32)
            for number in range(1, bulk_ref.shape[0]):
                match = classes == float(number)
                bulk = jnp.where(match, bulk_ref[number], bulk)
                shear = jnp.where(match, shear_ref[number], shear)
                dens = jnp.where(match, dens_ref[number], dens)
            inertia[r] = TIME_STEP / dens
            a_coef[r] = (9.0 / (VOLUME * VOLUME)) * (bulk - (5.0 / 3.0) * shear)
            stiff = (15.0 / VOLUME) * shear
            for c in range(-NEAR, NEAR + 1):
                b_shift[c + NEAR, r] = shifted(stiff, c)

    depth = lax.broadcasted_iota(jnp.int32, (cols, nz), 1)
    column = lax.broadcasted_iota(jnp.int32, (cols, nz), 0) + gy * cols

    def partner(buffer, i, a, b, c, own):
        if c > NEAR:
            return shifted(own, c)
        return buffer[c + NEAR, i + a, pl.ds(REACH + b, cols)]

    def bond_vector(i, a, b, c, own):
        y = []
        for comp in range(3):
            if c > NEAR:
                there = shifted(own[3][comp], c)
                if comp == 2:
                    there = there + float(c)
            else:
                there = u_shift[c + NEAR, comp, i + a, pl.ds(REACH + b, cols)]
            y.append(there - (own[0][a], own[1][b], own[2])[comp])
        return y

    def geometry(i, a, b, c, own):
        y0, y1, y2 = bond_vector(i, a, b, c, own)
        square = y0 * y0 + y1 * y1 + y2 * y2
        inverse = lax.rsqrt(square)
        return square * inverse, inverse

    def own_motion(i):
        mine = [wide_u[comp, i, REACH : REACH + cols] for comp in range(3)]
        by_row = {a: mine[0] - float(a) for a in range(REACH + 1)}
        by_col = {b: mine[1] - float(b) for b in range(-REACH, REACH + 1)}
        return (by_row, by_col, mine[2], mine)

    def back(values, c):
        return values if c == 0 else pltpu.roll(values, c % nz, axis=1)

    def order(t):
        return lax.rem(t + rows - REACH, rows)

    def send_done(t, stage, keys, plan, whole, pack, final):
        @pl.when(t == REACH - 1)
        def _():
            pack_sums(whole, pack, "C", final)
            start_all(stage, keys["C"], *plan)

        @pl.when(t == 2 * REACH - 1)
        def _():
            pack_sums(whole, pack, "A", final)
            start_all(stage, keys["A"], *plan)

    def weights():
        @pl.loop(0, rows)
        def _(i):
            lane_in = {
                c: jnp.where((depth + c >= 0) & (depth + c < nz), 1.0, 0.0)
                for c in range(-NEAR, REACH + 1)
            }
            for (a, b), members in GROUPS.items():
                row_in = (gx * rows + i + a) < grid_rows * rows
                plane = jnp.where(
                    (column + b >= 0) & (column + b < grid_cols * cols) & row_in, 1.0, 0.0
                )
                for k, c in members:
                    flag[k, i] = intact_ref[k, i].astype(F32) * (plane * lane_in[c])

    def prepare():
        @pl.loop(0, rows)
        def _(i):
            own_b = b_shift[NEAR, i, pl.ds(REACH, cols)]
            for k, (a, b, c) in enumerate(OFFSETS):
                both_b = own_b + partner(b_shift, i, a, b, c, own_b)
                scale = flag[k, i] * by_inverse[k, i]
                by_stretch[k, i] = scale * (both_b * (by_stretch[k, i] * (1.0 / RADII[k])))
                by_inverse[k, i] = scale

    def strain_pass(send):
        strain[...] = jnp.zeros(strain.shape, F32)

        @pl.loop(0, rows)
        def _(t):
            i = order(t)
            own = own_motion(i)
            sums = []
            for (a, b), members in GROUPS.items():
                returned = []
                for k, c in members:
                    length, inverse = geometry(i, a, b, c, own)
                    stretch = length - RADII[k]
                    by_inverse[k, i] = inverse
                    by_stretch[k, i] = stretch
                    term = flag[k, i] * stretch
                    sums.append(term)
                    returned.append(back(term, c))
                at = pl.ds(REACH + b, cols)
                strain[0, i + a, at] = strain[0, i + a, at] + tree_sum(returned)
                sums = [tree_sum(sums)]
            at = pl.ds(REACH, cols)
            strain[0, i, at] = strain[0, i, at] + sums[0]
            send(t)

    def force_pass(send):
        force[...] = jnp.zeros(force.shape, F32)

        @pl.loop(0, rows)
        def _(t):
            i = order(t)
            own = own_motion(i)
            mid = pl.ds(REACH, cols)
            own_a = a_shift[NEAR, i, mid]
            sums = [[], [], []]
            for (a, b), members in GROUPS.items():
                at = pl.ds(REACH + b, cols)
                returned = [[], [], []]
                for k, c in members:
                    y = bond_vector(i, a, b, c, own)
                    both_a = own_a + partner(a_shift, i, a, b, c, own_a)
                    tension = by_inverse[k, i] * both_a + by_stretch[k, i]
                    for comp in range(3):
                        term = tension * y[comp]
                        sums[comp].append(term)
                        returned[comp].append(back(term, c))
                for comp in range(3):
                    force[comp, i + a, at] = force[comp, i + a, at] - tree_sum(returned[comp])
                    sums[comp] = [tree_sum(sums[comp])]
            for comp in range(3):
                force[comp, i, mid] = force[comp, i, mid] + sums[comp][0]

            send(t)

    def pack_sums(whole, pack, chunk, final):
        first, end = rows_of[chunk]
        start = start_of[chunk]
        width = 3 if final else 6
        high = cols + REACH if final else cols
        for comp in range(whole.shape[0]):
            for n, r in enumerate(range(first, end)):
                at = start + width * n
                pack[0, comp, at : at + width] = whole[comp, r, 0:width]
                pack[1, comp, at : at + width] = whole[comp, r, high : high + width]

    def take_sums(stage, keys, plan, whole, comps, final):
        wait_sends(stage, [key for key in keys["C"] + keys["A"] if key[1][1] == 0], *plan)
        width = 3 if final else 6
        for key in keys["C"] + keys["A"] + keys["B"]:
            chunk, direction = key
            origin = (-direction[0], -direction[1])

            @pl.when(here[origin])
            def _(key=key, chunk=chunk, origin=origin):
                wait_recv(stage, key, *plan)
                dx, dy = origin
                buf = plan[1](key)
                first, end = rows_of[chunk]
                first = first + dx * rows
                for comp in range(comps):
                    for n in range(end - rows_of[chunk][0]):
                        if dy == 0:
                            whole[comp, first + n] = whole[comp, first + n] + buf[comp, n]
                            continue
                        low = REACH if final else 0
                        at = pl.ds(low if dy < 0 else cols, width)
                        whole[comp, first + n, at] = (
                            whole[comp, first + n, at] + buf[comp, width * n : width * n + width]
                        )

    def finish_sends(stage, keys, plan):
        rest = keys["C"] + keys["A"] + keys["B"]
        wait_sends(stage, [key for key in rest if key[1][1] != 0], *plan)

    for load in loads[3:]:
        load.wait()
    weights()
    take_state(0, u_plan, lambda comp: wide_u.at[comp], 3)
    shift_motion()

    for step in range(STEPS):
        last = step == STEPS - 1
        stage = 2 + 2 * step
        t_plan = (
            lambda key: sum_source(key, strain, pack_t, False),
            lambda key, step=step: sum_target(key, t_x, t_y, t_d, step, False),
        )
        strain_pass(
            lambda t, stage=stage, t_plan=t_plan: send_done(
                t, stage, CHUNKS, t_plan, strain, pack_t, False
            ),
        )
        pack_sums(strain, pack_t, "B", False)
        start_all(stage, CHUNKS["B"], *t_plan)
        if step == 0:
            take_state(1, vm_plan, lambda comp: wide_v.at[comp], 4)
            materials()
        prepare()
        take_sums(stage, CHUNKS, t_plan, strain, 1, False)

        @pl.loop(0, wide_rows)
        def _(r):
            values = strain[0, r] * a_coef[r]
            for c in range(-NEAR, NEAR + 1):
                a_shift[c + NEAR, r] = shifted(values, c)

        finish_sends(stage, CHUNKS, t_plan)
        stage = stage + 1
        keys = FINAL if last else CHUNKS
        f_plan = (
            lambda key, last=last: sum_source(key, force, pack_f, last),
            lambda key, step=step, last=last: sum_target(key, f_x, f_y, f_d, step, last),
        )
        force_pass(
            lambda t, stage=stage, keys=keys, f_plan=f_plan, last=last: send_done(
                t, stage, keys, f_plan, force, pack_f, last
            )
        )
        pack_sums(force, pack_f, "B", last)
        start_all(stage, keys["B"], *f_plan)
        take_sums(stage, keys, f_plan, force, 3, last)
        if not last:

            @pl.loop(0, wide_rows)
            def _(r):
                for comp in range(3):
                    speed = wide_v[comp, r] + force[comp, r] * inertia[r]
                    wide_v[comp, r] = speed
                    wide_u[comp, r] = wide_u[comp, r] + TIME_STEP * speed

            shift_motion()
            finish_sends(stage, keys, f_plan)
        else:
            mid = pl.ds(REACH, cols)

            @pl.loop(0, rows)
            def _(r):
                for comp in range(3):
                    pull = force[comp, r, mid]
                    speed = wide_v[comp, r, mid] + pull * inertia[r, mid]
                    out_f[comp, r] = pull
                    out_v[comp, r] = speed
                    out_u[comp, r] = wide_u[comp, r, mid] + TIME_STEP * speed

            finish_sends(stage, keys, f_plan)
            wait_sends(0, STATE, *u_plan)
            wait_sends(1, STATE, *vm_plan)


def hand_over(u_in, v_in, f_in, u_out, v_out, f_out):
    u_out[...] = u_in[...]
    v_out[...] = v_in[...]
    f_out[...] = f_in[...]


def on_device(displacement, velocity, intact, material, bulk_modulus, shear_modulus, density):
    rows, cols, nz = material.shape
    wide_rows = rows + REACH
    padded = round_up(cols + 2 * REACH, 8)
    packed = 2 * round_up(6 * REACH, 8) + round_up(6 * (rows - REACH), 8)
    own = jax.ShapeDtypeStruct((3, rows, cols, nz), F32)
    vmem = pl.BlockSpec(memory_space=pltpu.VMEM)
    hbm = pl.BlockSpec(memory_space=pltpu.HBM)
    table = pltpu.SMEM(bulk_modulus.shape, F32)
    stages = 2 + 2 * STEPS

    def buffer(*shape):
        return pltpu.VMEM(shape + (nz,), F32)

    results = pl.pallas_call(
        functools.partial(kernel, lax.axis_size("gx"), lax.axis_size("gy")),
        out_shape=(own, own, own),
        in_specs=[hbm] * 7,
        out_specs=(vmem, vmem, vmem),
        scratch_shapes=[
            buffer(3, rows, cols),
            pltpu.VMEM(material.shape, jnp.int32),
            table,
            table,
            table,
            pltpu.VMEM(intact.shape, jnp.int32),
            pltpu.VMEM(intact.shape, F32),
            pltpu.VMEM(intact.shape, F32),
            pltpu.VMEM(intact.shape, F32),
            buffer(3, wide_rows, padded),
            buffer(4, wide_rows, padded),
            buffer(5, 3, wide_rows, padded),
            buffer(5, wide_rows, padded),
            buffer(5, wide_rows, padded),
            buffer(wide_rows, padded),
            buffer(wide_rows, padded),
            buffer(1, wide_rows, padded),
            buffer(3, wide_rows, padded),
            buffer(4, rows, cols),
            buffer(2, 3, 3 * rows),
            buffer(2, 4, 3 * rows),
            buffer(2, 1, packed),
            buffer(2, 3, packed),
            buffer(3, REACH, cols),
            buffer(2, 3, 3 * rows),
            buffer(2, 3, 16),
            buffer(4, REACH, cols),
            buffer(2, 4, 3 * rows),
            buffer(2, 4, 16),
            buffer(STEPS, 2, 1, REACH, padded),
            buffer(STEPS, 2, 1, packed),
            buffer(STEPS, 4, 1, 24),
            buffer(STEPS, 2, 3, REACH, padded),
            buffer(STEPS, 2, 3, packed),
            buffer(STEPS, 4, 3, 24),
            pltpu.SemaphoreType.DMA((7,)),
            pltpu.SemaphoreType.DMA((stages, 12)),
            pltpu.SemaphoreType.DMA((stages, 12)),
        ],
        compiler_params=pltpu.CompilerParams(
            collective_id=0, has_side_effects=True, vmem_limit_bytes=67_043_328
        ),
        name="peridynamics",
    )(displacement, velocity, intact, material, bulk_modulus, shear_modulus, density)
    return pl.pallas_call(
        hand_over,
        out_shape=(own, own, own),
        in_specs=[vmem] * 3,
        out_specs=(vmem, vmem, vmem),
        name="hand_over",
    )(*results)


def solution(mesh):
    node = P(None, "gx", "gy", None)
    return jax.shard_map(
        on_device,
        mesh=mesh,
        in_specs=(node, node, node, P("gx", "gy", None), P(), P(), P()),
        out_specs=(node, node, node),
        check_vma=False,
    )
```

time: 55.1 us -> 44.9 us (0.81)
  the two profiles are of different devices: /device:TPU:9 before, /device:TPU:0 now
where the time goes in v2:
time: 44.9 us; the launch traced here: 44.7 us
  Pallas kernels  44.1 us (98%)
  between operations  0.64 us (1%)
    pallas_call x1, Pallas kernels, on_device(): pl.pallas_call(functools.partial(kernel, lax.axis_size('gx'), lax.axis_si...  42.4 us
    pallas_call x1, Pallas kernels, on_device(): pl.pallas_call(hand_over, out_shape=(own, own, own), in_specs=[vmem] * 3,...  1.7 us

profile of v2, /device:TPU:0, one launch (start us, length us, event | category | flops | bytes accessed | tf_op | source)
XLA Modules:
  0.0 44.7 jit_solution(17494570835006328346)
XLA Ops:
  0.6 42.4 %peridynamics.1 = (f32[3,8,8,128]{3,2,1,0:T(8,128)}, f32[3,8,8,128]{3,2,1,0:T(8,128)}, f32[3,8,8,128]{3,2,1,0:T(8,128)}) custom-call(f32[3,8,8,128]{3,2,1,0:T(8,128)} %u_hbm.1, f32[3,8,8,128]{3,2,1,0:T(8,128)} %v_hbm.1, s32[61,8,8,128]{3,2,1,0:T(8,128)} %intact_hbm.1, s32[8,8,128]{2,1,0:T(8,128)} %mat_hbm.1, f32[8]{0:T(128)} %bulk_hbm.1, f32[8]{0:T(128)} %shear_hbm.1, ...), custom_call_target="tpu_custom_call" | custom-call | tf_op jit(solution)/shard_map/peridynamics/pallas_call | solution.py:595
  43.0 1.7 %hand_over.1 = (f32[3,8,8,128]{3,2,1,0:T(8,128)}, f32[3,8,8,128]{3,2,1,0:T(8,128)}, f32[3,8,8,128]{3,2,1,0:T(8,128)}) custom-call(f32[3,8,8,128]{3,2,1,0:T(8,128)} %get-tuple-element.6.u_in, f32[3,8,8,128]{3,2,1,0:T(8,128)} %get-tuple-element.7.v_in, f32[3,8,8,128]{3,2,1,0:T(8,128)} %get-tuple-element.8.f_in), custom_call_target="tpu_custom_call" | custom-call | tf_op jit(solution)/shard_map/hand_over/pallas_call | solution.py:645
